TPU v7x, 32 devices: a whole 2x2x4 slice. The times are simulated.
32 devices in a mesh: dp: 4 (over y, x), vocab: 8 (over z, core).
Axes of the slice: x: 2, y: 2, z: 4, core: 2. Of those that a mesh axis runs over, the one named last changes fastest.
Arguments:
- token_ids: int32 [64, 512], P(('dp', 'vocab')), may hold values from 0 to 30719, as said below
- type_ids: int32 [64, 512], P(('dp', 'vocab')), may hold values from 0 to 1
- lengths: int32 [64], P(('dp', 'vocab')), may hold values from 20 to 512, as said below
- word_table: bfloat16 [30720, 768], P('vocab'), may hold values from -6 to 6
- pos_table: bfloat16 [512, 768], replicated, may hold values from -4 to 4
- token_type_embeddings: bfloat16 [2, 768], replicated, may hold values from -4 to 4
- emb_gain: float32 [768], replicated, may hold values from 0.25 to 1.75
- emb_bias: float32 [768], replicated, may hold values from -3 to 3
- query_weight: bfloat16 [768, 768], replicated, may hold values from -0.21875 to 0.21875
- query_bias: float32 [768], replicated, may hold values from -3 to 3
- key_weight: bfloat16 [768, 768], replicated, may hold values from -0.21875 to 0.21875
- value_weight: bfloat16 [768, 768], replicated, may hold values from -0.21875 to 0.21875
- value_bias: float32 [768], replicated, may hold values from -3 to 3
- out_weight: bfloat16 [768, 768], replicated, may hold values from -0.875 to 0.875
- out_bias: float32 [768], replicated, may hold values from -3 to 3
- attn_gain: float32 [768], replicated, may hold values from 0.25 to 1.75
- attn_bias: float32 [768], replicated, may hold values from -3 to 3
- up_weight: bfloat16 [768, 3072], replicated, may hold values from -0.21875 to 0.21875
- up_bias: float32 [3072], replicated, may hold values from -3 to 3
- down_weight: bfloat16 [3072, 768], replicated, may hold values from -0.109375 to 0.109375
- down_bias: float32 [768], replicated, may hold values from -3 to 3
- final_gain: float32 [768], replicated, may hold values from 0.25 to 1.75
- final_bias: float32 [768], replicated, may hold values from -3 to 3
- cotangent: bfloat16 [64, 512, 768], P(('dp', 'vocab')), may hold values from -6 to 6
Outputs:
- encoded: float32 [64, 512, 768], P(('dp', 'vocab'))
- word_grad: float32 [30720, 768], P('vocab')
- pos_grad: float32 [512, 768], P('vocab')
- type_grad: float32 [2, 768], P(None, 'vocab')
- emb_gain_grad: float32 [768], P('vocab')
- emb_bias_grad: float32 [768], P('vocab')
- query_weight_grad: float32 [768, 768], P('vocab')
- query_bias_grad: float32 [768], P('vocab')
- key_weight_grad: float32 [768, 768], P('vocab')
- value_weight_grad: float32 [768, 768], P('vocab')
- value_bias_grad: float32 [768], P('vocab')
- out_weight_grad: float32 [768, 768], P('vocab')
- out_bias_grad: float32 [768], P('vocab')
- attn_gain_grad: float32 [768], P('vocab')
- attn_bias_grad: float32 [768], P('vocab')
- up_weight_grad: float32 [768, 3072], P('vocab')
- up_bias_grad: float32 [3072], P('vocab')
- down_weight_grad: float32 [3072, 768], P('vocab')
- down_bias_grad: float32 [768], P('vocab')
- final_gain_grad: float32 [768], P('vocab')
- final_bias_grad: float32 [768], P('vocab')
Inputs may be any that keep to these rules, and one draw needn't show every extreme that they name: `token_ids`: among the tokens of one device, at most 256 ids fall into the 3840 rows of word_table that one index of vocab holds; for one such block of rows, the same on every device, exactly 256 do. `lengths`: the tokens at positions from a sequence's length on are padding; some sequence has length 512 and some 20.
All inputs are finite; a program needn't handle non-finite values.
Results may differ from a plain program's by a relative error of at most 0.017.
Values may be sent and summed in bfloat16 or wider, within the bound.
A program may use at most 192 MiB of HBM per device.

v0:
```python
from functools import partial
import jax
import jax.numpy as jnp
from jax import lax
from jax.sharding import PartitionSpec as P

HEADS = 12
HEAD = 64
L = 512
EPSILON = 1e-12


def layer_norm(values, gain, bias):
    center = values - jnp.mean(values, -1, keepdims=True)
    spread = jnp.mean(center * center, -1, keepdims=True)
    return center * lax.rsqrt(spread + EPSILON) * gain + bias


def matmul(left, right):
    return jnp.dot(left, right, preferred_element_type=jnp.float32)


def matmul_tn(left, right):
    return lax.dot_general(
        left, right, (((0,), (0,)), ((), ())), preferred_element_type=jnp.float32
    )


def matmul_nt(left, right):
    return lax.dot_general(
        left, right, (((1,), (1,)), ((), ())), preferred_element_type=jnp.float32
    )


def masked_scores(query, keys, length):
    scores = jnp.einsum("qhd,khd->hqk", query, keys, preferred_element_type=jnp.float32) * HEAD ** (
        -0.5
    )
    visible = jnp.arange(L) < length
    return jnp.where(visible[None, None, :], scores, -1000000000.0)


def attend_forward(block):
    query, keys, values, length = block
    scores = masked_scores(query, keys, length)
    highest = jnp.max(scores, -1, keepdims=True)
    expd = jnp.exp(scores - highest)
    totals = jnp.sum(expd, -1, keepdims=True)
    probs_low = (expd / totals).astype(jnp.bfloat16)
    mixed = jnp.einsum("hqk,khd->qhd", probs_low, values, preferred_element_type=jnp.float32)
    return (mixed.astype(jnp.bfloat16), highest + jnp.log(totals))


def attend_backward(block):
    query, keys, values, grad_mixed, logsum, length = block
    probs = jnp.exp(masked_scores(query, keys, length) - logsum)
    probs_low = probs.astype(jnp.bfloat16)
    grad_values = jnp.einsum(
        "hqk,qhd->khd", probs_low, grad_mixed, preferred_element_type=jnp.float32
    )
    grad_probs = jnp.einsum("qhd,khd->hqk", grad_mixed, values, preferred_element_type=jnp.float32)
    inner = jnp.sum(grad_probs * probs, -1, keepdims=True)
    grad_scores = (probs * (grad_probs - inner)).astype(jnp.bfloat16)
    scale = HEAD ** (-0.5)
    grad_query = (
        jnp.einsum("hqk,khd->qhd", grad_scores, keys, preferred_element_type=jnp.float32) * scale
    )
    grad_keys = (
        jnp.einsum("hqk,qhd->khd", grad_scores, query, preferred_element_type=jnp.float32) * scale
    )
    return (grad_query, grad_keys, grad_values)


def swap(value, axis_name, bit):
    size = lax.axis_size(axis_name)
    return lax.ppermute(value, axis_name, [(i, i ^ bit) for i in range(size)])


def pick(value, index, axis):
    return lax.dynamic_index_in_dim(value, index, axis, keepdims=False)


def plus(left, right):
    return (left.astype(jnp.float32) + right.astype(jnp.float32)).astype(jnp.bfloat16)


def dp_bits():
    index = lax.axis_index("dp")
    return (lax.rem(index, 2), index // 2)


def reorder(own, across_x, across_y, across_both):
    xb, yb = dp_bits()
    flip_x, flip_y = (xb == 1, yb == 1)
    rows = [[own, across_y], [across_x, across_both]]
    rows = [[jnp.where(flip_x, rows[1 - i][j], rows[i][j]) for j in range(2)] for i in range(2)]
    rows = [[jnp.where(flip_y, rows[i][1 - j], rows[i][j]) for j in range(2)] for i in range(2)]
    return rows


def sum_over_all(grad):
    size = lax.axis_size("vocab")
    me = lax.axis_index("vocab")
    core = lax.rem(me, 2)
    place = me // 2
    places = size // 2
    total, n = grad.shape
    r = total // size
    xb, yb = dp_bits()
    grad = grad.reshape(places, 2, r, n)
    other = swap(pick(grad, 1 - core, 1), "vocab", 1)
    held = plus(pick(grad, core, 1), other).reshape(places, 2, 2, r // 4, n)
    first, last = (held[: places // 2], held[places // 2 :])
    first_in = swap(pick(first, 1 - xb, 1), "dp", 1)
    last_in = swap(pick(last, 1 - yb, 2), "dp", 2)
    first = plus(pick(first, xb, 1), first_in)
    last = plus(pick(last, yb, 2), last_in)
    first_in = swap(pick(first, 1 - yb, 1), "dp", 2)
    last_in = swap(pick(last, 1 - xb, 1), "dp", 1)
    first = plus(pick(first, yb, 1), first_in)
    last = plus(pick(last, xb, 1), last_in)
    held = jnp.concatenate([first, last], 0)
    summed = pick(held, place, 0).astype(jnp.float32)
    for step in range(1, places):
        block = pick(held, lax.rem(place + step, places), 0)
        block = lax.ppermute(block, "vocab", [(i, (i + 2 * step) % size) for i in range(size)])
        summed = summed + block.astype(jnp.float32)
    own = summed.astype(jnp.bfloat16)
    across_x = swap(own, "dp", 1)
    across_y = swap(own, "dp", 2)
    half = n // 2
    both = jnp.concatenate(
        [swap(across_x[:, :half], "dp", 2), swap(across_y[:, half:], "dp", 1)], 1
    )
    rows = reorder(own, across_x, across_y, both)
    return (
        jnp.stack([rows[0][0], rows[0][1], rows[1][0], rows[1][1]])
        .reshape(r, n)
        .astype(jnp.float32)
    )


def sum_over_dp(grad):
    rows, n = grad.shape
    xb, yb = dp_bits()
    held = grad.reshape(2, 2, 2, rows // 8, n)
    first, last = (held[0], held[1])
    first_in = swap(pick(first, 1 - xb, 0), "dp", 1)
    last_in = swap(pick(last, 1 - yb, 1), "dp", 2)
    first = plus(pick(first, xb, 0), first_in)
    last = plus(pick(last, yb, 1), last_in)
    first_in = swap(pick(first, 1 - yb, 0), "dp", 2)
    last_in = swap(pick(last, 1 - xb, 0), "dp", 1)
    first = plus(pick(first, yb, 0), first_in)
    last = plus(pick(last, xb, 0), last_in)
    first_x = swap(first, "dp", 1)
    last_y = swap(last, "dp", 2)
    first_y = swap(jnp.stack([first, first_x]), "dp", 2)
    last_x = swap(jnp.stack([last, last_y]), "dp", 1)
    a = reorder(first, first_x, first_y[0], first_y[1])
    b = reorder(last, last_x[0], last_y, last_x[1])
    parts = [p for group in (a, b) for line in group for p in line]
    return jnp.concatenate(parts, 0).astype(jnp.float32)


def local(
    token_ids,
    type_ids,
    lengths,
    word_table,
    pos_table,
    token_type_embeddings,
    emb_gain,
    emb_bias,
    query_weight,
    query_bias,
    key_weight,
    value_weight,
    value_bias,
    out_weight,
    out_bias,
    attn_gain,
    attn_bias,
    up_weight,
    up_bias,
    down_weight,
    down_bias,
    final_gain,
    final_bias,
    cotangent,
):
    seq_count, seq_len = token_ids.shape
    tokens = seq_count * seq_len
    width = word_table.shape[1]
    rows_local = word_table.shape[0]
    owners = lax.axis_size("vocab")
    capacity = max(2, 2 * tokens // owners)
    flat_ids = token_ids.reshape(tokens)
    owner = flat_ids // rows_local
    member = (owner[:, None] == jnp.arange(owners)[None, :]).astype(jnp.int32)
    earlier = jnp.cumsum(member, 0) - member
    rank = jnp.sum(earlier * member, 1)
    slot = owner * capacity + rank
    requests = (
        jnp.full((owners * capacity,), -1, jnp.int32).at[slot].set(flat_ids - owner * rows_local)
    )
    requests = requests.reshape(owners, capacity)
    asked = lax.all_to_all(requests, "vocab", split_axis=0, concat_axis=0, tiled=True)
    valid = asked >= 0
    found = word_table[jnp.maximum(asked, 0)]
    found = jnp.where(valid[..., None], found, jnp.zeros((), jnp.bfloat16))
    returned = lax.all_to_all(found, "vocab", split_axis=0, concat_axis=0, tiled=True)
    word_rows = returned.reshape(owners * capacity, width)[slot]
    kinds = token_type_embeddings.shape[0]
    selection_matrix = (type_ids[..., None] == jnp.arange(kinds)[None, None, :]).astype(jnp.float32)
    type_rows = jnp.einsum(
        "tcr,rb->tcb",
        selection_matrix,
        token_type_embeddings.astype(jnp.float32),
        precision=lax.Precision.HIGHEST,
    )
    embedded = (
        word_rows.reshape(seq_count, seq_len, width).astype(jnp.float32)
        + pos_table.astype(jnp.float32)[None]
        + type_rows
    )
    normed = layer_norm(embedded, emb_gain, emb_bias).reshape(tokens, width)
    normed_low = normed.astype(jnp.bfloat16)
    query = (matmul(normed_low, query_weight) + query_bias).astype(jnp.bfloat16)
    keys = matmul(normed_low, key_weight).astype(jnp.bfloat16)
    values = (matmul(normed_low, value_weight) + value_bias).astype(jnp.bfloat16)
    split_shape = (seq_count, seq_len, HEADS, HEAD)
    query_split = query.reshape(split_shape)
    keys_split = keys.reshape(split_shape)
    values_split = values.reshape(split_shape)
    mixed, logsum = lax.map(attend_forward, (query_split, keys_split, values_split, lengths))
    mixed_low = mixed.reshape(tokens, width)
    first = normed + matmul(mixed_low, out_weight) + out_bias
    hidden = layer_norm(first, attn_gain, attn_bias)
    hidden_reduced_precision = hidden.astype(jnp.bfloat16)
    upper = matmul(hidden_reduced_precision, up_weight) + up_bias
    active_low = jax.nn.gelu(upper, approximate=False).astype(jnp.bfloat16)
    second = hidden + matmul(active_low, down_weight) + down_bias
    encoded = layer_norm(second, final_gain, final_bias)
    grad_out = cotangent.reshape(tokens, width).astype(jnp.float32)
    _, final_pull = jax.vjp(layer_norm, second, final_gain, final_bias)
    grad_second, grad_final_gain, grad_final_bias = final_pull(grad_out)
    grad_down_bias = jnp.sum(grad_second, 0)
    second_matmul_gradient_reduced = grad_second.astype(jnp.bfloat16)
    grad_down = matmul_tn(active_low, second_matmul_gradient_reduced)
    grad_active = matmul_nt(second_matmul_gradient_reduced, down_weight)
    _, gelu_pull = jax.vjp(partial(jax.nn.gelu, approximate=False), upper)
    (grad_upper,) = gelu_pull(grad_active)
    grad_up_bias = jnp.sum(grad_upper, 0)
    grad_upper_low = grad_upper.astype(jnp.bfloat16)
    grad_up = matmul_tn(hidden_reduced_precision, grad_upper_low)
    grad_hidden = grad_second + matmul_nt(grad_upper_low, up_weight)
    _, attn_pull = jax.vjp(layer_norm, first, attn_gain, attn_bias)
    grad_first, grad_attn_gain, grad_attn_bias = attn_pull(grad_hidden)
    grad_out_bias = jnp.sum(grad_first, 0)
    grad_first_low = grad_first.astype(jnp.bfloat16)
    grad_out_weight = matmul_tn(mixed_low, grad_first_low)
    grad_mixed = matmul_nt(grad_first_low, out_weight).astype(jnp.bfloat16)
    grad_query, grad_keys, grad_values = lax.map(
        attend_backward,
        (query_split, keys_split, values_split, grad_mixed.reshape(split_shape), logsum, lengths),
    )
    grad_query = grad_query.reshape(tokens, width)
    grad_keys = grad_keys.reshape(tokens, width)
    grad_values = grad_values.reshape(tokens, width)
    grad_query_bias = jnp.sum(grad_query, 0)
    grad_value_bias = jnp.sum(grad_values, 0)
    grad_query_low = grad_query.astype(jnp.bfloat16)
    grad_keys_low = grad_keys.astype(jnp.bfloat16)
    grad_values_low = grad_values.astype(jnp.bfloat16)
    grad_query_weight = matmul_tn(normed_low, grad_query_low)
    grad_key_weight = matmul_tn(normed_low, grad_keys_low)
    grad_value_weight = matmul_tn(normed_low, grad_values_low)
    grad_normed = (
        grad_first
        + matmul_nt(grad_query_low, query_weight)
        + matmul_nt(grad_keys_low, key_weight)
        + matmul_nt(grad_values_low, value_weight)
    )
    _, emb_pull = jax.vjp(layer_norm, embedded, emb_gain, emb_bias)
    embedding_output_gradient, grad_emb_gain, grad_emb_bias = emb_pull(
        grad_normed.reshape(seq_count, seq_len, width)
    )
    grad_pos = jnp.sum(embedding_output_gradient, 0)
    token_type_gradient = jnp.einsum(
        "nox,noh->xh", selection_matrix, embedding_output_gradient, precision=lax.Precision.HIGHEST
    )
    bf = jnp.bfloat16
    per = width // owners
    grad_down_all = sum_over_all(grad_down.astype(bf))
    grad_up_all = sum_over_all(grad_up.astype(bf))
    places = slot[None, :] == jnp.arange(owners * capacity)[:, None]
    outgoing = matmul(
        places.astype(bf), embedding_output_gradient.reshape(tokens, width).astype(bf)
    ).astype(bf)
    hits = (jnp.arange(rows_local)[:, None] == asked.reshape(-1)[None, :]).astype(bf)
    pieces = []
    step = 256
    for start in range(0, width, step):
        incoming = lax.all_to_all(
            outgoing[:, start : start + step].reshape(owners, capacity, step),
            "vocab",
            split_axis=0,
            concat_axis=0,
            tiled=True,
        )
        dense = matmul(hits, incoming.reshape(owners * capacity, step)).astype(bf)
        pieces.append(sum_over_dp(dense))
    grad_word = jnp.concatenate(pieces, 1)
    small = jnp.stack(
        [
            grad_query_bias,
            grad_value_bias,
            grad_out_bias,
            grad_attn_gain,
            grad_attn_bias,
            grad_emb_gain,
            grad_emb_bias,
            grad_down_bias,
            grad_final_gain,
            grad_final_bias,
            token_type_gradient[0],
            token_type_gradient[1],
        ]
    )
    small = small.reshape(12, owners, per).transpose(1, 0, 2).reshape(owners, 12 * per)
    small = jnp.concatenate([small, grad_up_bias.reshape(owners, 4 * per)], 1)
    wide = 4 * width
    lines = seq_len // owners * width // wide
    rest = per // 3 - lines
    small_lines = jnp.pad(small, ((0, 0), (0, rest * wide - 16 * per))).reshape(owners, rest, wide)
    mixed_grads = jnp.concatenate(
        [grad_query_weight, grad_key_weight, grad_value_weight, grad_out_weight], 1
    ).astype(bf)
    packed = jnp.concatenate(
        [
            mixed_grads.reshape(owners, per, wide),
            grad_pos.astype(bf).reshape(owners, lines, wide),
            small_lines.astype(bf),
        ],
        1,
    )
    packed = sum_over_all(packed.reshape(-1, wide))
    weights = packed[:per]
    grad_query_weight = weights[:, :width]
    grad_key_weight = weights[:, width : 2 * width]
    grad_value_weight = weights[:, 2 * width : 3 * width]
    grad_out_weight = weights[:, 3 * width :]
    grad_pos = packed[per : per + lines].reshape(seq_len // owners, width)
    small = packed[per + lines :].reshape(-1)[: 16 * per].reshape(16, per)
    (
        grad_query_bias,
        grad_value_bias,
        grad_out_bias,
        grad_attn_gain,
        grad_attn_bias,
        grad_emb_gain,
        grad_emb_bias,
        grad_down_bias,
        grad_final_gain,
        grad_final_bias,
    ) = [small[i] for i in range(10)]
    token_type_gradient = small[10:12]
    grad_up_bias = small[12:].reshape(-1)
    grad_up, grad_down = (grad_up_all, grad_down_all)
    return (
        encoded.reshape(seq_count, seq_len, width),
        grad_word,
        grad_pos,
        token_type_gradient,
        grad_emb_gain,
        grad_emb_bias,
        grad_query_weight,
        grad_query_bias,
        grad_key_weight,
        grad_value_weight,
        grad_value_bias,
        grad_out_weight,
        grad_out_bias,
        grad_attn_gain,
        grad_attn_bias,
        grad_up,
        grad_up_bias,
        grad_down,
        grad_down_bias,
        grad_final_gain,
        grad_final_bias,
    )


def solution(mesh):
    placed = (
        P(("dp", "vocab"), None),
        P(("dp", "vocab"), None),
        P(("dp", "vocab")),
        P("vocab", None),
        P(),
        P(),
        P(),
        P(),
        P(),
        P(),
        P(),
        P(),
        P(),
        P(),
        P(),
        P(),
        P(),
        P(),
        P(),
        P(),
        P(),
        P(),
        P(),
        P(("dp", "vocab"), None, None),
    )
    return jax.shard_map(
        local,
        mesh=mesh,
        in_specs=placed,
        out_specs=(
            P(("dp", "vocab"), None, None),
            P("vocab", None),
            P("vocab", None),
            P(None, "vocab"),
            P("vocab"),
            P("vocab"),
            P("vocab", None),
            P("vocab"),
            P("vocab", None),
            P("vocab", None),
            P("vocab"),
            P("vocab", None),
            P("vocab"),
            P("vocab"),
            P("vocab"),
            P("vocab", None),
            P("vocab"),
            P("vocab", None),
            P("vocab"),
            P("vocab"),
            P("vocab"),
        ),
        check_vma=False,
    )
```

profile of v0, /device:TPU:0, one launch (start us, length us, event | category | flops | bytes accessed | tf_op | source)
XLA Modules:
  0.0 785.7 jit_solution(7070408737902939160)
XLA Ops:
  7.8 4.3 scatter_custom_fusion
  12.1 11.7 %all_to_all.29 = s32[8,1,256]{2,1,0:T(1,128)S(1)} all-to-all(s32[8,1,256]{2,1,0:T(1,128)S(1)} %bitcast.728), channel_id=1, replica_groups=mesh['dp'=4,'vocab'=8] {'vocab'}, dimensions={0} | all-to-all | bytes 16384 | tf_op jit(solution)/shard_map/all_to_all | solution.py:208
  23.9 13.5 %gather_fusion = bf16[2048,768]{1,0:T(8,128)(2,1)} fusion(bf16[3840,768]{1,0:T(8,128)(2,1)} %param.31, s32[2048]{0:T(1024)S(1)} %broadcast_clamp_fusion), kind=kCustom, calls=%fused_computation | custom fusion | bytes 6299648 | tf_op jit(solution)/shard_map/gather | solution.py:210
  37.4 3.3 broadcast_select_fusion
  40.7 5.1 all-to-all-start.1
  48.2 69.1 %all-to-all-done.1 = bf16[8,256,768]{2,1,0:T(8,128)(2,1)} async-done(((bf16[8,256,768]{2,1,0:T(8,128)(2,1)}), bf16[8,256,768]{2,1,0:T(8,128)(2,1)}, u32[]{:S(2)}, u32[]{:S(2)}) %all-to-all-start.1) | async-done | bytes 3145760 | tf_op jit(solution)/shard_map/all_to_all | solution.py:212
  117.3 8.0 %gather_fusion.1 = bf16[1024,768]{1,0:T(8,128)(2,1)} fusion(bf16[2048,768]{1,0:T(8,128)(2,1)} %bitcast.25, s32[1024]{0:T(1024)S(1)} %broadcast_clamp_fusion.1), kind=kCustom, calls=%fused_computation.1 | custom fusion | bytes 3149824 | tf_op jit(solution)/shard_map/gather | solution.py:213
  157.3 3.9 reshape.625
  164.0 25.6 %while.26 = (s32[]{:T(128)}, bf16[2,512,12,64]{1,3,2,0:T(8,128)(2,1)}, f32[2,12,512,1]{2,1,3,0:T(8,128)}, bf16[2,512,12,64]{1,3,2,0:T(8,128)(2,1)}, s32[2]{0:T(1...) while((s32[]{:T(128)}, ...), condition=%wide.region_9.10_spmd, body=%wide.region_6.9_spmd.sunk | while | flops 843442688 | bytes 47411840 | solution.py:236
  165.4 4.1 fusion.269
  172.7 4.2 fusion.271
  178.1 4.1 fusion.269
  185.4 4.2 fusion.271
  189.6 3.6 copy.214
  198.1 35.1 %multiply_convert_fusion.1 = (bf16[1024,3072]{1,0:T(8,128)(2,1)S(1)}, f32[1024,3072]{1,0:T(8,128)}, f32[1024,3072]{1,0:T(8,128)}) fusion(f32[3072]{0:T(1024)S(1)} %copy-done.82, bf16[768,3072]{1,0:T(8,128)(2,1)S(1)} %bitcast.738, f32[1024,768]{1,0:T(8,128)S(1)} %get-tuple-element.331, f32[768]{0:T(1024)S(1)} %copy-done.87, f32[768]{0:T(1024)S(1)} %copy-done.73, ...), kind=kOutput, calls=%fused_computation.69 | convolution fusion | flops 5043388416 | bytes 39348224 | tf_op jit(solution)/shard_map/dot_general | solution.py:20
  233.2 5.5 fusion.215
  244.9 7.7 convolution_convert_fusion
  252.6 19.4 %fusion.216 = (bf16[3072]{0:T(1024)(128)(2,1)}, bf16[1024,3072]{1,0:T(8,128)(2,1)}) fusion(f32[1024,3072]{1,0:T(8,128)} %get-tuple-element.251, bf16[3072,768]{1,0:T(8,128)(2,1)} %param.47, f32[1024,768]{1,0:T(8,128)} %copy-done.21, f32[1024]{0:T(1024)S(1)} %negate_multiply_fusion.3, f32[1024,3072]{1,0:T(8,128)} %get-tuple-element.332, f32[3072]{0:T(1024)S(1)} %copy-done.82), kind=kOutput, calls=%fused_computation.487 | convolution fusion | flops 4883739648 | bytes 39344128 | tf_op jit(solution)/shard_map/dot_general | solution.py:30
  272.1 10.7 %convolution_convert_fusion.1 = bf16[768,3072]{1,0:T(8,128)(2,1)} fusion(bf16[1024,3072]{1,0:T(8,128)(2,1)} %get-tuple-element.337, f32[1024,768]{1,0:T(8,128)} %copy-done.19, f32[768]{0:T(1024)S(1)} %copy-done.87, f32[768]{0:T(1024)S(1)} %copy-done.73, f32[1024]{0:T(1024)S(1)} %fusion.191, f32[1024]{0:T(1024)S(1)} %broadcast_multiply_fusion.1), kind=kOutput, calls=%fused_computation.93 | convolution fusion | flops 4838129664 | bytes 14170112 | tf_op jit(solution)/shard_map/dot_general | solution.py:24
  282.8 8.9 %multiply_reduce_fusion.2 = (bf16[768]{0:T(1024)(128)(2,1)}, f32[1024]{0:T(1024)S(1)}, bf16[768]{0:T(1024)(128)(2,1)}, f32[1024,768]{1,0:T(8,128)S(1)}) fusion(f32[1024,768]{1,0:T(8,128)S(1)} %copy-done.20, f32[1024]{0:T(1024)S(1)} %fusion.191, f32[1024]{0:T(1024)S(1)} %broadcast_multiply_fusion.1, f32[768]{0:T(1024)S(1)} %copy-done.73, ...), kind=kOutput, calls=%fused_computation.116 | convolution fusion | flops 4839699456 | bytes 20469760 | tf_op jit(solution)/shard_map/dot_general | solution.py:30
  298.2 4.0 reshape.628
  305.1 55.7 %while.27 = (s32[]{:T(128)}, f32[2,512,12,64]{1,3,2,0:T(8,128)}, bf16[2,512,12,64]{1,3,2,0:T(8,128)(2,1)}, f32[2,512,12,64]{1,3,2,0:T(8,128)}, bf16[2,512,12,64]...) while((s32[]{:T(128)}, f32[2,512,12,64]{1,3,2,0:T(8,128)}, ...), condition=%wide.region_20.21_spmd, body=%wide.region_18.20_spmd.sunk | while | flops 2061232640 | bytes 161414480 | solution.py:264
  305.4 3.1 fusion.280
  309.8 7.3 multiply_reduce_fusion.9
  317.1 7.4 multiply_convert_fusion.3
  329.0 3.9 bitcast_dynamic-update-slice_fusion.11
  337.4 7.3 multiply_reduce_fusion.9
  344.7 7.4 multiply_convert_fusion.3
  356.7 4.0 bitcast_dynamic-update-slice_fusion.11
  360.9 5.5 fusion.203
  385.0 3.3 fusion.113
  389.9 3.3 dynamic-slice_bitcast_fusion.2
  396.5 5.4 fusion.68
  403.7 4.4 all-to-all-start.2
  412.6 4.0 fusion.100
  424.1 10.6 %all-to-all-done.2 = bf16[8,256,256]{2,1,0:T(8,128)(2,1)} async-done(((bf16[8,256,256]{2,1,0:T(8,128)(2,1)}), bf16[8,256,256]{2,1,0:T(8,128)(2,1)}, u32[]{:S(2)}, u32[]{:S(2)}) %all-to-all-start.2) | async-done | bytes 1048608 | tf_op jit(solution)/shard_map/all_to_all | solution.py:305
  434.7 4.2 all-to-all-start.3
  446.0 8.2 %fusion.60 = bf16[3840,256]{1,0:T(8,128)(2,1)} fusion(bf16[2048,256]{1,0:T(8,128)(2,1)} %bitcast.35, s32[2048]{0:T(1024)S(1)} %bitcast.722), kind=kOutput, calls=%fused_computation.89 | convolution fusion | flops 4035379200 | bytes 3022848 | tf_op jit(solution)/shard_map/dot_general | solution.py:20
  454.3 11.3 %all-to-all-done.3 = bf16[8,256,256]{2,1,0:T(8,128)(2,1)} async-done(((bf16[8,256,256]{2,1,0:T(8,128)(2,1)}), bf16[8,256,256]{2,1,0:T(8,128)(2,1)}, u32[]{:S(2)}, u32[]{:S(2)}) %all-to-all-start.3) | async-done | bytes 1048608 | tf_op jit(solution)/shard_map/all_to_all | solution.py:305
  465.5 4.5 all-to-all-start.4
  474.0 7.2 fusion.61
  483.7 12.9 %all-to-all-done.4 = bf16[8,256,256]{2,1,0:T(8,128)(2,1)} async-done(((bf16[8,256,256]{2,1,0:T(8,128)(2,1)}), bf16[8,256,256]{2,1,0:T(8,128)(2,1)}, u32[]{:S(2)}, u32[]{:S(2)}) %all-to-all-start.4) | async-done | bytes 1048608 | tf_op jit(solution)/shard_map/all_to_all | solution.py:305
  496.6 7.5 fusion.62
  509.7 8.9 %collective-permute-done = bf16[2,480,256]{2,1,0:T(8,128)(2,1)S(1)} collective-permute-done((bf16[2,480,256]{2,1,0:T(8,128)(2,1)S(1)}, bf16[2,480,256]{2,1,0:T(8,128)(2,1)S(1)}, u32[]{:S(2)}, u32[]{:S(2)}) %collective-permute-start) | collective-permute-done | bytes 491552 | tf_op jit(solution)/shard_map/ppermute | solution.py:76
  520.3 7.5 collective-permute-done.8
  530.8 11.2 %collective-permute-done.16 = bf16[2,480,256]{2,1,0:T(8,128)(2,1)S(1)} collective-permute-done((bf16[2,480,256]{2,1,0:T(8,128)(2,1)S(1)}, bf16[2,480,256]{2,1,0:T(8,128)(2,1)S(1)}, u32[]{:S(2)}, u32[]{:S(2)}) %collective-permute-start.16) | collective-permute-done | bytes 491552 | tf_op jit(solution)/shard_map/ppermute | solution.py:76
  562.8 26.9 %collective-permute-done.6 = bf16[480,256]{1,0:T(8,128)(2,1)S(1)} collective-permute-done((bf16[480,256]{1,0:T(8,128)(2,1)S(1)}, bf16[480,256]{1,0:T(8,128)(2,1)S(1)}, u32[]{:S(2)}, u32[]{:S(2)}) %collective-permute-start.6) | collective-permute-done | bytes 245792 | tf_op jit(solution)/shard_map/ppermute | solution.py:76
  592.2 5.5 collective-permute-done.14
  601.0 3.1 collective-permute-done.22
  611.6 9.0 %collective-permute-done.49 = bf16[2,2,96,768]{3,2,0,1:T(8,128)(2,1)S(1)} collective-permute-done((bf16[2,2,96,768]{3,2,0,1:T(8,128)(2,1)S(1)}, bf16[2,2,96,768]{3,2,0,1:T(8,128)(2,1)S(1)}, u32[]{:S(2)}, u32[]{:S(2)}) %collective-permute-start.49) | collective-permute-done | bytes 589856 | tf_op jit(solution)/shard_map/ppermute | solution.py:76
  622.7 10.5 %collective-permute-done.37 = bf16[2,2,24,3072]{3,2,0,1:T(8,128)(2,1)S(1)} collective-permute-done((bf16[2,2,24,3072]{3,2,0,1:T(8,128)(2,1)S(1)}, bf16[2,2,24,3072]{3,2,0,1:T(8,128)(2,1)S(1)}, u32[]{:S(2)}, u32[]{:S(2)}) %collective-permute-start.37) | collective-permute-done | bytes 589856 | tf_op jit(solution)/shard_map/ppermute | solution.py:76
  639.1 23.7 %collective-permute-done.40 = bf16[2,24,3072]{2,1,0:T(8,128)(2,1)S(1)} collective-permute-done((bf16[2,24,3072]{2,1,0:T(8,128)(2,1)S(1)}, bf16[2,24,3072]{2,1,0:T(8,128)(2,1)S(1)}, u32[]{:S(2)}, u32[]{:S(2)}) %collective-permute-start.40) | collective-permute-done | bytes 294944 | tf_op jit(solution)/shard_map/ppermute | solution.py:76
  663.6 8.5 %collective-permute-done.38 = bf16[2,24,3072]{2,1,0:T(8,128)(2,1)S(1)} collective-permute-done((bf16[2,24,3072]{2,1,0:T(8,128)(2,1)S(1)}, bf16[2,24,3072]{2,1,0:T(8,128)(2,1)S(1)}, u32[]{:S(2)}, u32[]{:S(2)}) %collective-permute-start.38) | collective-permute-done | bytes 294944 | tf_op jit(solution)/shard_map/ppermute | solution.py:76
  674.4 7.7 collective-permute-done.50
  687.1 5.5 collective-permute-done.11
  694.2 9.0 %collective-permute-done.19 = bf16[2,480,256]{2,1,0:T(8,128)(2,1)S(1)} collective-permute-done((bf16[2,480,256]{2,1,0:T(8,128)(2,1)S(1)}, bf16[2,480,256]{2,1,0:T(8,128)(2,1)S(1)}, u32[]{:S(2)}, u32[]{:S(2)}) %collective-permute-start.19) | collective-permute-done | bytes 491552 | tf_op jit(solution)/shard_map/ppermute | solution.py:76
  709.5 5.5 collective-permute-start.55
  723.0 4.8 maximum_convert_fusion
  731.2 14.4 %collective-permute-done.47 = bf16[24,1536]{1,0:T(8,128)(2,1)S(1)} collective-permute-done((bf16[24,1536]{1,0:T(8,128)(2,1)S(1)}, bf16[24,1536]{1,0:T(8,128)(2,1)S(1)}, u32[]{:S(2)}, u32[]{:S(2)}) %collective-permute-start.47) | collective-permute-done | bytes 73760 | tf_op jit(solution)/shard_map/ppermute | solution.py:76
  748.6 6.4 collective-permute-done.28
  755.7 4.8 collective-permute-start.30
  760.5 3.1 collective-permute-done.29
  763.7 4.2 collective-permute-done.30
  770.1 4.0 collective-permute-done.32
  (583 shorter events, 234.4 us)
Async XLA Ops:
  40.7 76.7 %all-to-all-start.1 = ((bf16[8,256,768]{2,1,0:T(8,128)(2,1)}), bf16[8,256,768]{2,1,0:T(8,128)(2,1)}, u32[]{:S(2)}, u32[]{:S(2)}) async-start(bf16[8,256,768]{2,1,0:T(8,128)(2,1)} %broadcast_select_fusion), calls=%async_computation.1 | async-start | bytes 6291456 | tf_op jit(solution)/shard_map/all_to_all | solution.py:212
  393.2 150.5 %collective-permute-start.48 = (bf16[4,384,768]{2,1,0:T(8,128)(2,1)}, bf16[4,384,768]{2,1,0:T(8,128)(2,1)}, u32[]{:S(2)}, u32[]{:S(2)}) collective-permute-start(bf16[4,384,768]{2,1,0:T(8,128)(2,1)} %dynamic-slice_bitcast_fusion.2), channel_id=1, source_target_pairs={{0,1},{1,0},{2,3},{3,2},{4,5},{5,4},{6,7},{7,6},{8,9},{9,8},{10,11... | collective-permute-start | bytes 7077896 | tf_op jit(solution)/shard_map/ppermute | solution.py:76
  394.9 152.7 %collective-permute-start.36 = (bf16[4,96,3072]{2,1,0:T(8,128)(2,1)}, bf16[4,96,3072]{2,1,0:T(8,128)(2,1)}, u32[]{:S(2)}, u32[]{:S(2)}) collective-permute-start(bf16[4,96,3072]{2,1,0:T(8,128)(2,1)} %dynamic-slice_bitcast_fusion.3), channel_id=1, source_target_pairs={{0,1},{1,0},{2,3},{3,2},{4,5},{5,4},{6,7},{7,6},{8,9},{9,8},{10,11... | collective-permute-start | bytes 7077896 | tf_op jit(solution)/shard_map/ppermute | solution.py:76
  403.7 31.0 %all-to-all-start.2 = ((bf16[8,256,256]{2,1,0:T(8,128)(2,1)}), bf16[8,256,256]{2,1,0:T(8,128)(2,1)}, u32[]{:S(2)}, u32[]{:S(2)}) async-start(bf16[8,256,256]{2,1,0:T(8,128)(2,1)} %bitcast.34), calls=%async_computation.2 | async-start | bytes 2097152 | tf_op jit(solution)/shard_map/all_to_all | solution.py:305
  434.7 30.8 %all-to-all-start.3 = ((bf16[8,256,256]{2,1,0:T(8,128)(2,1)}), bf16[8,256,256]{2,1,0:T(8,128)(2,1)}, u32[]{:S(2)}, u32[]{:S(2)}) async-start(bf16[8,256,256]{2,1,0:T(8,128)(2,1)} %bitcast.54), calls=%async_computation.3 | async-start | bytes 2097152 | tf_op jit(solution)/shard_map/all_to_all | solution.py:305
  445.7 189.6 %collective-permute-start.24 = (bf16[4,128,3072]{2,1,0:T(8,128)(2,1)}, bf16[4,128,3072]{2,1,0:T(8,128)(2,1)}, u32[]{:S(2)}, u32[]{:S(2)}) collective-permute-start(bf16[4,128,3072]{2,1,0:T(8,128)(2,1)} %dynamic-slice_bitcast_fusion.1), channel_id=1, source_target_pairs={{0,1},{1,0},{2,3},{3,2},{4,5},{5,4},{6,7},{7,6},{8,9},{9,8},{10,11... | collective-permute-start | bytes 9437192 | tf_op jit(solution)/shard_map/ppermute | solution.py:76
  465.5 31.1 %all-to-all-start.4 = ((bf16[8,256,256]{2,1,0:T(8,128)(2,1)}), bf16[8,256,256]{2,1,0:T(8,128)(2,1)}, u32[]{:S(2)}, u32[]{:S(2)}) async-start(bf16[8,256,256]{2,1,0:T(8,128)(2,1)} %bitcast.74), calls=%async_computation.4 | async-start | bytes 2097152 | tf_op jit(solution)/shard_map/all_to_all | solution.py:305
  472.5 31.9 %collective-permute-start.4 = (bf16[2,480,256]{2,1,0:T(8,128)(2,1)}, bf16[2,480,256]{2,1,0:T(8,128)(2,1)}, u32[]{:S(2)}, u32[]{:S(2)}) collective-permute-start(bf16[2,480,256]{2,1,0:T(8,128)(2,1)} %dynamic-slice_bitcast_fusion.9), channel_id=1, source_target_pairs={{0,16},{8,24},{16,0},{24,8},{1,17},{9,25},{17,1},{25,9},{2,18},{10... | collective-permute-start | bytes 1474568 | tf_op jit(solution)/shard_map/ppermute | solution.py:76
  483.2 24.0 %collective-permute-start.12 = (bf16[2,480,256]{2,1,0:T(8,128)(2,1)}, bf16[2,480,256]{2,1,0:T(8,128)(2,1)}, u32[]{:S(2)}, u32[]{:S(2)}) collective-permute-start(bf16[2,480,256]{2,1,0:T(8,128)(2,1)} %dynamic-slice_bitcast_fusion.7), channel_id=1, source_target_pairs={{0,16},{8,24},{16,0},{24,8},{1,17},{9,25},{17,1},{25,9},{2,18},{10... | collective-permute-start | bytes 1474568 | tf_op jit(solution)/shard_map/ppermute | solution.py:76
  504.4 14.2 %collective-permute-start = (bf16[2,480,256]{2,1,0:T(8,128)(2,1)S(1)}, bf16[2,480,256]{2,1,0:T(8,128)(2,1)S(1)}, u32[]{:S(2)}, u32[]{:S(2)}) collective-permute-start(bf16[2,480,256]{2,1,0:T(8,128)(2,1)S(1)} %dynamic-slice_bitcast_fusion.10), channel_id=1, source_target_pairs={{0,8},{8,0},{16,24},{24,16},{1,9},{9,1},{17,25},{25,17},{2,10},{10... | collective-permute-start | bytes 1474568 | tf_op jit(solution)/shard_map/ppermute | solution.py:76
  507.2 20.6 %collective-permute-start.8 = (bf16[2,480,256]{2,1,0:T(8,128)(2,1)S(1)}, bf16[2,480,256]{2,1,0:T(8,128)(2,1)S(1)}, u32[]{:S(2)}, u32[]{:S(2)}) collective-permute-start(bf16[2,480,256]{2,1,0:T(8,128)(2,1)S(1)} %dynamic-slice_bitcast_fusion.8), channel_id=1, source_target_pairs={{0,8},{8,0},{16,24},{24,16},{1,9},{9,1},{17,25},{25,17},{2,10},{10... | collective-permute-start | bytes 1474568 | tf_op jit(solution)/shard_map/ppermute | solution.py:76
  518.7 10.8 %collective-permute-start.20 = (bf16[2,480,256]{2,1,0:T(8,128)(2,1)S(1)}, bf16[2,480,256]{2,1,0:T(8,128)(2,1)S(1)}, u32[]{:S(2)}, u32[]{:S(2)}) collective-permute-start(bf16[2,480,256]{2,1,0:T(8,128)(2,1)S(1)} %dynamic-slice_bitcast_fusion.5), channel_id=1, source_target_pairs={{0,16},{8,24},{16,0},{24,8},{1,17},{9,25},{17,1},{25,9},{2,18},{10... | collective-permute-start | bytes 1474568 | tf_op jit(solution)/shard_map/ppermute | solution.py:76
  527.8 14.2 %collective-permute-start.16 = (bf16[2,480,256]{2,1,0:T(8,128)(2,1)S(1)}, bf16[2,480,256]{2,1,0:T(8,128)(2,1)S(1)}, u32[]{:S(2)}, u32[]{:S(2)}) collective-permute-start(bf16[2,480,256]{2,1,0:T(8,128)(2,1)S(1)} %dynamic-slice_bitcast_fusion.6), channel_id=1, source_target_pairs={{0,8},{8,0},{16,24},{24,16},{1,9},{9,1},{17,25},{25,17},{2,10},{10... | collective-permute-start | bytes 1474568 | tf_op jit(solution)/shard_map/ppermute | solution.py:76
  529.5 22.0 %collective-permute-start.5 = (bf16[480,256]{1,0:T(8,128)(2,1)S(1)}, bf16[480,256]{1,0:T(8,128)(2,1)S(1)}, u32[]{:S(2)}, u32[]{:S(2)}) collective-permute-start(bf16[480,256]{1,0:T(8,128)(2,1)S(1)} %dynamic-slice_bitcast_fusion.21), channel_id=1, source_target_pairs={{0,8},{8,0},{16,24},{24,16},{1,9},{9,1},{17,25},{25,17},{2,10},{10... | collective-permute-start | bytes 737288 | tf_op jit(solution)/shard_map/ppermute | solution.py:76
  542.0 10.3 %collective-permute-start.1 = (bf16[480,256]{1,0:T(8,128)(2,1)S(1)}, bf16[480,256]{1,0:T(8,128)(2,1)S(1)}, u32[]{:S(2)}, u32[]{:S(2)}) collective-permute-start(bf16[480,256]{1,0:T(8,128)(2,1)S(1)} %dynamic-slice_bitcast_fusion.22), channel_id=1, source_target_pairs={{0,16},{8,24},{16,0},{24,8},{1,17},{9,25},{17,1},{25,9},{2,18},{10... | collective-permute-start | bytes 737288 | tf_op jit(solution)/shard_map/ppermute | solution.py:76
  543.7 10.2 %collective-permute-start.13 = (bf16[480,256]{1,0:T(8,128)(2,1)S(1)}, bf16[480,256]{1,0:T(8,128)(2,1)S(1)}, u32[]{:S(2)}, u32[]{:S(2)}) collective-permute-start(bf16[480,256]{1,0:T(8,128)(2,1)S(1)} %dynamic-slice_bitcast_fusion.19), channel_id=1, source_target_pairs={{0,8},{8,0},{16,24},{24,16},{1,9},{9,1},{17,25},{25,17},{2,10},{10... | collective-permute-start | bytes 737288 | tf_op jit(solution)/shard_map/ppermute | solution.py:76
  547.6 9.0 %collective-permute-start.9 = (bf16[480,256]{1,0:T(8,128)(2,1)S(1)}, bf16[480,256]{1,0:T(8,128)(2,1)S(1)}, u32[]{:S(2)}, u32[]{:S(2)}) collective-permute-start(bf16[480,256]{1,0:T(8,128)(2,1)S(1)} %dynamic-slice_bitcast_fusion.20), channel_id=1, source_target_pairs={{0,16},{8,24},{16,0},{24,8},{1,17},{9,25},{17,1},{25,9},{2,18},{10... | collective-permute-start | bytes 737288 | tf_op jit(solution)/shard_map/ppermute | solution.py:76
  551.6 6.3 collective-permute-start.21
  552.2 9.6 %collective-permute-start.17 = (bf16[480,256]{1,0:T(8,128)(2,1)S(1)}, bf16[480,256]{1,0:T(8,128)(2,1)S(1)}, u32[]{:S(2)}, u32[]{:S(2)}) collective-permute-start(bf16[480,256]{1,0:T(8,128)(2,1)S(1)} %dynamic-slice_bitcast_fusion.18), channel_id=1, source_target_pairs={{0,16},{8,24},{16,0},{24,8},{1,17},{9,25},{17,1},{25,9},{2,18},{10... | collective-permute-start | bytes 737288 | tf_op jit(solution)/shard_map/ppermute | solution.py:76
  553.9 56.0 %collective-permute-start.51 = (bf16[2,2,96,768]{3,2,0,1:T(8,128)(2,1)S(1)}, bf16[2,2,96,768]{3,2,0,1:T(8,128)(2,1)S(1)}, u32[]{:S(2)}, u32[]{:S(2)}) collective-permute-start(bf16[2,2,96,768]{3,2,0,1:T(8,128)(2,1)S(1)} %bitcast.717), channel_id=1, source_target_pairs={{0,16},{8,24},{16,0},{24,8},{1,17},{9,25},{17,1},{25,9},{2,18},{10... | collective-permute-start | bytes 1769480 | tf_op jit(solution)/shard_map/ppermute | solution.py:76
  556.6 53.6 %collective-permute-start.39 = (bf16[2,2,24,3072]{3,2,0,1:T(8,128)(2,1)S(1)}, bf16[2,2,24,3072]{3,2,0,1:T(8,128)(2,1)S(1)}, u32[]{:S(2)}, u32[]{:S(2)}) collective-permute-start(bf16[2,2,24,3072]{3,2,0,1:T(8,128)(2,1)S(1)} %bitcast.716), channel_id=1, source_target_pairs={{0,16},{8,24},{16,0},{24,8},{1,17},{9,25},{17,1},{25,9},{2,18},{10... | collective-permute-start | bytes 1769480 | tf_op jit(solution)/shard_map/ppermute | solution.py:76
  557.9 31.8 %collective-permute-start.6 = (bf16[480,256]{1,0:T(8,128)(2,1)S(1)}, bf16[480,256]{1,0:T(8,128)(2,1)S(1)}, u32[]{:S(2)}, u32[]{:S(2)}) collective-permute-start(bf16[480,256]{1,0:T(8,128)(2,1)S(1)} %fusion.133), channel_id=1, source_target_pairs={{0,16},{8,24},{16,0},{24,8},{1,17},{9,25},{17,1},{25,9},{2,18},{10... | collective-permute-start | bytes 737288 | tf_op jit(solution)/shard_map/ppermute | solution.py:76
  561.9 28.6 %collective-permute-start.2 = (bf16[480,256]{1,0:T(8,128)(2,1)S(1)}, bf16[480,256]{1,0:T(8,128)(2,1)S(1)}, u32[]{:S(2)}, u32[]{:S(2)}) collective-permute-start(bf16[480,256]{1,0:T(8,128)(2,1)S(1)} %fusion.134), channel_id=1, source_target_pairs={{0,8},{8,0},{16,24},{24,16},{1,9},{9,1},{17,25},{25,17},{2,10},{10... | collective-permute-start | bytes 737288 | tf_op jit(solution)/shard_map/ppermute | solution.py:76
  589.7 8.1 %collective-permute-start.14 = (bf16[480,256]{1,0:T(8,128)(2,1)S(1)}, bf16[480,256]{1,0:T(8,128)(2,1)S(1)}, u32[]{:S(2)}, u32[]{:S(2)}) collective-permute-start(bf16[480,256]{1,0:T(8,128)(2,1)S(1)} %fusion.131), channel_id=1, source_target_pairs={{0,16},{8,24},{16,0},{24,8},{1,17},{9,25},{17,1},{25,9},{2,18},{10... | collective-permute-start | bytes 737288 | tf_op jit(solution)/shard_map/ppermute | solution.py:76
  590.5 8.6 %collective-permute-start.10 = (bf16[480,256]{1,0:T(8,128)(2,1)S(1)}, bf16[480,256]{1,0:T(8,128)(2,1)S(1)}, u32[]{:S(2)}, u32[]{:S(2)}) collective-permute-start(bf16[480,256]{1,0:T(8,128)(2,1)S(1)} %fusion.132), channel_id=1, source_target_pairs={{0,8},{8,0},{16,24},{24,16},{1,9},{9,1},{17,25},{25,17},{2,10},{10... | collective-permute-start | bytes 737288 | tf_op jit(solution)/shard_map/ppermute | solution.py:76
  597.7 6.4 collective-permute-start.22
  599.1 8.9 %collective-permute-start.18 = (bf16[480,256]{1,0:T(8,128)(2,1)S(1)}, bf16[480,256]{1,0:T(8,128)(2,1)S(1)}, u32[]{:S(2)}, u32[]{:S(2)}) collective-permute-start(bf16[480,256]{1,0:T(8,128)(2,1)S(1)} %fusion.130), channel_id=1, source_target_pairs={{0,8},{8,0},{16,24},{24,16},{1,9},{9,1},{17,25},{25,17},{2,10},{10... | collective-permute-start | bytes 737288 | tf_op jit(solution)/shard_map/ppermute | solution.py:76
  604.1 16.5 %collective-permute-start.49 = (bf16[2,2,96,768]{3,2,0,1:T(8,128)(2,1)S(1)}, bf16[2,2,96,768]{3,2,0,1:T(8,128)(2,1)S(1)}, u32[]{:S(2)}, u32[]{:S(2)}) collective-permute-start(bf16[2,2,96,768]{3,2,0,1:T(8,128)(2,1)S(1)} %bitcast.715), channel_id=1, source_target_pairs={{0,8},{8,0},{16,24},{24,16},{1,9},{9,1},{17,25},{25,17},{2,10},{10... | collective-permute-start | bytes 1769480 | tf_op jit(solution)/shard_map/ppermute | solution.py:76
  607.9 25.3 %collective-permute-start.37 = (bf16[2,2,24,3072]{3,2,0,1:T(8,128)(2,1)S(1)}, bf16[2,2,24,3072]{3,2,0,1:T(8,128)(2,1)S(1)}, u32[]{:S(2)}, u32[]{:S(2)}) collective-permute-start(bf16[2,2,24,3072]{3,2,0,1:T(8,128)(2,1)S(1)} %bitcast.714), channel_id=1, source_target_pairs={{0,8},{8,0},{16,24},{24,16},{1,9},{9,1},{17,25},{25,17},{2,10},{10... | collective-permute-start | bytes 1769480 | tf_op jit(solution)/shard_map/ppermute | solution.py:76
  609.9 76.1 %collective-permute-start.7 = (bf16[2,480,256]{2,1,0:T(8,128)(2,1)S(1)}, bf16[2,480,256]{2,1,0:T(8,128)(2,1)S(1)}, u32[]{:S(2)}, u32[]{:S(2)}) collective-permute-start(bf16[2,480,256]{2,1,0:T(8,128)(2,1)S(1)} %pad_maximum_fusion.5), channel_id=1, source_target_pairs={{0,8},{8,0},{16,24},{24,16},{1,9},{9,1},{17,25},{25,17},{2,10},{10... | collective-permute-start | bytes 1474568 | tf_op jit(solution)/shard_map/ppermute | solution.py:76
  610.3 73.6 %collective-permute-start.3 = (bf16[2,480,256]{2,1,0:T(8,128)(2,1)S(1)}, bf16[2,480,256]{2,1,0:T(8,128)(2,1)S(1)}, u32[]{:S(2)}, u32[]{:S(2)}) collective-permute-start(bf16[2,480,256]{2,1,0:T(8,128)(2,1)S(1)} %pad_maximum_fusion.4), channel_id=1, source_target_pairs={{0,16},{8,24},{16,0},{24,8},{1,17},{9,25},{17,1},{25,9},{2,18},{10... | collective-permute-start | bytes 1474568 | tf_op jit(solution)/shard_map/ppermute | solution.py:76
  620.6 72.6 %collective-permute-start.15 = (bf16[2,480,256]{2,1,0:T(8,128)(2,1)S(1)}, bf16[2,480,256]{2,1,0:T(8,128)(2,1)S(1)}, u32[]{:S(2)}, u32[]{:S(2)}) collective-permute-start(bf16[2,480,256]{2,1,0:T(8,128)(2,1)S(1)} %pad_maximum_fusion.7), channel_id=1, source_target_pairs={{0,8},{8,0},{16,24},{24,16},{1,9},{9,1},{17,25},{25,17},{2,10},{10... | collective-permute-start | bytes 1474568 | tf_op jit(solution)/shard_map/ppermute | solution.py:76
  633.2 40.1 %collective-permute-start.52 = (bf16[2,96,768]{2,1,0:T(8,128)(2,1)S(1)}, bf16[2,96,768]{2,1,0:T(8,128)(2,1)S(1)}, u32[]{:S(2)}, u32[]{:S(2)}) collective-permute-start(bf16[2,96,768]{2,1,0:T(8,128)(2,1)S(1)} %dynamic-slice_bitcast_fusion.13), channel_id=1, source_target_pairs={{0,8},{8,0},{16,24},{24,16},{1,9},{9,1},{17,25},{25,17},{2,10},{10... | collective-permute-start | bytes 884744 | tf_op jit(solution)/shard_map/ppermute | solution.py:76
  635.3 27.5 %collective-permute-start.40 = (bf16[2,24,3072]{2,1,0:T(8,128)(2,1)S(1)}, bf16[2,24,3072]{2,1,0:T(8,128)(2,1)S(1)}, u32[]{:S(2)}, u32[]{:S(2)}) collective-permute-start(bf16[2,24,3072]{2,1,0:T(8,128)(2,1)S(1)} %dynamic-slice_bitcast_fusion.15), channel_id=1, source_target_pairs={{0,8},{8,0},{16,24},{24,16},{1,9},{9,1},{17,25},{25,17},{2,10},{10... | collective-permute-start | bytes 884744 | tf_op jit(solution)/shard_map/ppermute | solution.py:76
  662.8 9.3 %collective-permute-start.38 = (bf16[2,24,3072]{2,1,0:T(8,128)(2,1)S(1)}, bf16[2,24,3072]{2,1,0:T(8,128)(2,1)S(1)}, u32[]{:S(2)}, u32[]{:S(2)}) collective-permute-start(bf16[2,24,3072]{2,1,0:T(8,128)(2,1)S(1)} %dynamic-slice_bitcast_fusion.16), channel_id=1, source_target_pairs={{0,16},{8,24},{16,0},{24,8},{1,17},{9,25},{17,1},{25,9},{2,18},{10... | collective-permute-start | bytes 884744 | tf_op jit(solution)/shard_map/ppermute | solution.py:76
  672.1 9.9 %collective-permute-start.50 = (bf16[2,96,768]{2,1,0:T(8,128)(2,1)S(1)}, bf16[2,96,768]{2,1,0:T(8,128)(2,1)S(1)}, u32[]{:S(2)}, u32[]{:S(2)}) collective-permute-start(bf16[2,96,768]{2,1,0:T(8,128)(2,1)S(1)} %dynamic-slice_bitcast_fusion.14), channel_id=1, source_target_pairs={{0,16},{8,24},{16,0},{24,8},{1,17},{9,25},{17,1},{25,9},{2,18},{10... | collective-permute-start | bytes 884744 | tf_op jit(solution)/shard_map/ppermute | solution.py:76
  673.4 19.3 %collective-permute-start.11 = (bf16[2,480,256]{2,1,0:T(8,128)(2,1)S(1)}, bf16[2,480,256]{2,1,0:T(8,128)(2,1)S(1)}, u32[]{:S(2)}, u32[]{:S(2)}) collective-permute-start(bf16[2,480,256]{2,1,0:T(8,128)(2,1)S(1)} %pad_maximum_fusion.6), channel_id=1, source_target_pairs={{0,16},{8,24},{16,0},{24,8},{1,17},{9,25},{17,1},{25,9},{2,18},{10... | collective-permute-start | bytes 1474568 | tf_op jit(solution)/shard_map/ppermute | solution.py:76
  682.1 21.7 %collective-permute-start.23 = (bf16[2,480,256]{2,1,0:T(8,128)(2,1)S(1)}, bf16[2,480,256]{2,1,0:T(8,128)(2,1)S(1)}, u32[]{:S(2)}, u32[]{:S(2)}) collective-permute-start(bf16[2,480,256]{2,1,0:T(8,128)(2,1)S(1)} %pad_maximum_fusion.9), channel_id=1, source_target_pairs={{0,8},{8,0},{16,24},{24,16},{1,9},{9,1},{17,25},{25,17},{2,10},{10... | collective-permute-start | bytes 1474568 | tf_op jit(solution)/shard_map/ppermute | solution.py:76
  683.9 19.3 %collective-permute-start.19 = (bf16[2,480,256]{2,1,0:T(8,128)(2,1)S(1)}, bf16[2,480,256]{2,1,0:T(8,128)(2,1)S(1)}, u32[]{:S(2)}, u32[]{:S(2)}) collective-permute-start(bf16[2,480,256]{2,1,0:T(8,128)(2,1)S(1)} %pad_maximum_fusion.8), channel_id=1, source_target_pairs={{0,16},{8,24},{16,0},{24,8},{1,17},{9,25},{17,1},{25,9},{2,18},{10... | collective-permute-start | bytes 1474568 | tf_op jit(solution)/shard_map/ppermute | solution.py:76
  686.0 60.9 %collective-permute-start.27 = (bf16[2,2,32,3072]{3,2,1,0:T(8,128)(2,1)S(1)}, bf16[2,2,32,3072]{3,2,1,0:T(8,128)(2,1)S(1)}, u32[]{:S(2)}, u32[]{:S(2)}) collective-permute-start(bf16[2,2,32,3072]{3,2,1,0:T(8,128)(2,1)S(1)} %dynamic-slice_bitcast_fusion.4), channel_id=1, source_target_pairs={{0,16},{8,24},{16,0},{24,8},{1,17},{9,25},{17,1},{25,9},{2,18},{10... | collective-permute-start | bytes 2359304 | tf_op jit(solution)/shard_map/ppermute | solution.py:76
  692.6 22.6 %collective-permute-start.53 = (bf16[96,768]{1,0:T(8,128)(2,1)S(1)}, bf16[96,768]{1,0:T(8,128)(2,1)S(1)}, u32[]{:S(2)}, u32[]{:S(2)}) collective-permute-start(bf16[96,768]{1,0:T(8,128)(2,1)S(1)} %get-tuple-element.306), channel_id=1, source_target_pairs={{0,2},{1,3},{2,4},{3,5},{4,6},{5,7},{6,0},{7,1},{8,10},{9,11},{10,... | collective-permute-start | bytes 442376 | tf_op jit(solution)/shard_map/ppermute | solution.py:126
  693.2 12.0 %collective-permute-start.41 = (bf16[24,3072]{1,0:T(8,128)(2,1)S(1)}, bf16[24,3072]{1,0:T(8,128)(2,1)S(1)}, u32[]{:S(2)}, u32[]{:S(2)}) collective-permute-start(bf16[24,3072]{1,0:T(8,128)(2,1)S(1)} %get-tuple-element.313), channel_id=1, source_target_pairs={{0,2},{1,3},{2,4},{3,5},{4,6},{5,7},{6,0},{7,1},{8,10},{9,11},{10,... | collective-permute-start | bytes 442376 | tf_op jit(solution)/shard_map/ppermute | solution.py:126
  703.2 6.4 collective-permute-start.42
  703.8 11.3 %collective-permute-start.43 = (bf16[24,3072]{1,0:T(8,128)(2,1)S(1)}, bf16[24,3072]{1,0:T(8,128)(2,1)S(1)}, u32[]{:S(2)}, u32[]{:S(2)}) collective-permute-start(bf16[24,3072]{1,0:T(8,128)(2,1)S(1)} %get-tuple-element.315), channel_id=1, source_target_pairs={{0,6},{1,7},{2,0},{3,1},{4,2},{5,3},{6,4},{7,5},{8,14},{9,15},{10,... | collective-permute-start | bytes 442376 | tf_op jit(solution)/shard_map/ppermute | solution.py:126
  705.2 10.0 %collective-permute-start.54 = (bf16[96,768]{1,0:T(8,128)(2,1)S(1)}, bf16[96,768]{1,0:T(8,128)(2,1)S(1)}, u32[]{:S(2)}, u32[]{:S(2)}) collective-permute-start(bf16[96,768]{1,0:T(8,128)(2,1)S(1)} %get-tuple-element.307), channel_id=1, source_target_pairs={{0,4},{1,5},{2,6},{3,7},{4,0},{5,1},{6,2},{7,3},{8,12},{9,13},{10,... | collective-permute-start | bytes 442376 | tf_op jit(solution)/shard_map/ppermute | solution.py:126
  709.5 8.2 %collective-permute-start.55 = (bf16[96,768]{1,0:T(8,128)(2,1)S(1)}, bf16[96,768]{1,0:T(8,128)(2,1)S(1)}, u32[]{:S(2)}, u32[]{:S(2)}) collective-permute-start(bf16[96,768]{1,0:T(8,128)(2,1)S(1)} %get-tuple-element.308), channel_id=1, source_target_pairs={{0,6},{1,7},{2,0},{3,1},{4,2},{5,3},{6,4},{7,5},{8,14},{9,15},{10,... | collective-permute-start | bytes 442376 | tf_op jit(solution)/shard_map/ppermute | solution.py:126
  715.1 6.9 collective-permute-start.44
  717.8 10.0 %collective-permute-start.56 = (bf16[96,768]{1,0:T(8,128)(2,1)S(1)}, bf16[96,768]{1,0:T(8,128)(2,1)S(1)}, u32[]{:S(2)}, u32[]{:S(2)}) collective-permute-start(bf16[96,768]{1,0:T(8,128)(2,1)S(1)} %fusion.140), channel_id=1, source_target_pairs={{0,8},{8,0},{16,24},{24,16},{1,9},{9,1},{17,25},{25,17},{2,10},{10... | collective-permute-start | bytes 442376 | tf_op jit(solution)/shard_map/ppermute | solution.py:76
  717.9 9.9 %collective-permute-start.58 = (bf16[96,768]{1,0:T(8,128)(2,1)S(1)}, bf16[96,768]{1,0:T(8,128)(2,1)S(1)}, u32[]{:S(2)}, u32[]{:S(2)}) collective-permute-start(bf16[96,768]{1,0:T(8,128)(2,1)S(1)} %fusion.140), channel_id=1, source_target_pairs={{0,16},{8,24},{16,0},{24,8},{1,17},{9,25},{17,1},{25,9},{2,18},{10... | collective-permute-start | bytes 442376 | tf_op jit(solution)/shard_map/ppermute | solution.py:76
  718.9 10.1 %collective-permute-start.46 = (bf16[24,3072]{1,0:T(8,128)(2,1)S(1)}, bf16[24,3072]{1,0:T(8,128)(2,1)S(1)}, u32[]{:S(2)}, u32[]{:S(2)}) collective-permute-start(bf16[24,3072]{1,0:T(8,128)(2,1)S(1)} %fusion.143), channel_id=1, source_target_pairs={{0,16},{8,24},{16,0},{24,8},{1,17},{9,25},{17,1},{25,9},{2,18},{10... | collective-permute-start | bytes 442376 | tf_op jit(solution)/shard_map/ppermute | solution.py:76
  722.0 9.0 %collective-permute-start.45 = (bf16[24,1536]{1,0:T(8,128)(2,1)S(1)}, bf16[24,1536]{1,0:T(8,128)(2,1)S(1)}, u32[]{:S(2)}, u32[]{:S(2)}) collective-permute-start(bf16[24,1536]{1,0:T(8,128)(2,1)S(1)} %slice.326), channel_id=1, source_target_pairs={{0,16},{8,24},{16,0},{24,8},{1,17},{9,25},{17,1},{25,9},{2,18},{10... | collective-permute-start | bytes 221192 | tf_op jit(solution)/shard_map/ppermute | solution.py:76
  727.8 19.4 %collective-permute-start.25 = (bf16[2,2,32,3072]{3,2,0,1:T(8,128)(2,1)S(1)}, bf16[2,2,32,3072]{3,2,0,1:T(8,128)(2,1)S(1)}, u32[]{:S(2)}, u32[]{:S(2)}) collective-permute-start(bf16[2,2,32,3072]{3,2,0,1:T(8,128)(2,1)S(1)} %bitcast.713), channel_id=1, source_target_pairs={{0,8},{8,0},{16,24},{24,16},{1,9},{9,1},{17,25},{25,17},{2,10},{10... | collective-permute-start | bytes 2359304 | tf_op jit(solution)/shard_map/ppermute | solution.py:76
  727.8 32.7 %collective-permute-start.57 = (bf16[96,384]{1,0:T(8,128)(2,1)S(1)}, bf16[96,384]{1,0:T(8,128)(2,1)S(1)}, u32[]{:S(2)}, u32[]{:S(2)}) collective-permute-start(bf16[96,384]{1,0:T(8,128)(2,1)S(1)} %slice.331), channel_id=1, source_target_pairs={{0,16},{8,24},{16,0},{24,8},{1,17},{9,25},{17,1},{25,9},{2,18},{10... | collective-permute-start | bytes 221192 | tf_op jit(solution)/shard_map/ppermute | solution.py:76
  729.0 31.5 %collective-permute-start.59 = (bf16[96,384]{1,0:T(8,128)(2,1)S(1)}, bf16[96,384]{1,0:T(8,128)(2,1)S(1)}, u32[]{:S(2)}, u32[]{:S(2)}) collective-permute-start(bf16[96,384]{1,0:T(8,128)(2,1)S(1)} %slice.332), channel_id=1, source_target_pairs={{0,8},{8,0},{16,24},{24,16},{1,9},{9,1},{17,25},{25,17},{2,10},{10... | collective-permute-start | bytes 221192 | tf_op jit(solution)/shard_map/ppermute | solution.py:76
  731.1 14.5 %collective-permute-start.47 = (bf16[24,1536]{1,0:T(8,128)(2,1)S(1)}, bf16[24,1536]{1,0:T(8,128)(2,1)S(1)}, u32[]{:S(2)}, u32[]{:S(2)}) collective-permute-start(bf16[24,1536]{1,0:T(8,128)(2,1)S(1)} %slice.327), channel_id=1, source_target_pairs={{0,8},{8,0},{16,24},{24,16},{1,9},{9,1},{17,25},{25,17},{2,10},{10... | collective-permute-start | bytes 221192 | tf_op jit(solution)/shard_map/ppermute | solution.py:76
  747.1 7.8 collective-permute-start.28
  747.4 7.8 collective-permute-start.26
  755.6 8.1 %collective-permute-start.29 = (bf16[32,3072]{1,0:T(8,128)(2,1)S(1)}, bf16[32,3072]{1,0:T(8,128)(2,1)S(1)}, u32[]{:S(2)}, u32[]{:S(2)}) collective-permute-start(bf16[32,3072]{1,0:T(8,128)(2,1)S(1)} %get-tuple-element.299), channel_id=1, source_target_pairs={{0,2},{1,3},{2,4},{3,5},{4,6},{5,7},{6,0},{7,1},{8,10},{9,11},{10,... | collective-permute-start | bytes 589832 | tf_op jit(solution)/shard_map/ppermute | solution.py:126
  755.7 12.2 %collective-permute-start.30 = (bf16[32,3072]{1,0:T(8,128)(2,1)S(1)}, bf16[32,3072]{1,0:T(8,128)(2,1)S(1)}, u32[]{:S(2)}, u32[]{:S(2)}) collective-permute-start(bf16[32,3072]{1,0:T(8,128)(2,1)S(1)} %get-tuple-element.300), channel_id=1, source_target_pairs={{0,4},{1,5},{2,6},{3,7},{4,0},{5,1},{6,2},{7,3},{8,12},{9,13},{10,... | collective-permute-start | bytes 589832 | tf_op jit(solution)/shard_map/ppermute | solution.py:126
  760.5 7.7 collective-permute-start.31
  768.3 5.7 collective-permute-start.32
  768.9 7.4 collective-permute-start.34
  774.1 4.7 collective-permute-start.33
  776.4 4.7 collective-permute-start.35
  (111 other events, 909.6 us)
where the time goes:
time: 790 us; the launch traced here: 786 us
  waiting for transfers between devices  292 us (37%)
  matrix products  200 us (25%)
  local copies, waits for them, and re-layouts  108 us (14%)
  other arithmetic  86.7 us (11%)
  starting transfers between devices  82.7 us (10%)
  blocking collectives  11.7 us (1%)
    ppermute x51, waiting for transfers between devices, swap(): return lax.ppermute(value, axis_name, [(i, i ^ bit) for i in range(size)])  176 us
    dot_general x10, matrix products, matmul(): return jnp.dot(left, right, preferred_element_type=jnp.float32)  78.2 us
    all_to_all x1, waiting for transfers between devices, local(): lax.all_to_all(found, 'vocab', split_axis=0, concat_axis=0, tiled=True)  69.1 us
    ppermute x51, starting transfers between devices, swap(): return lax.ppermute(value, axis_name, [(i, i ^ bit) for i in range(size)])  50.7 us
    dot_general x6, matrix products, matmul_nt(): lax.dot_general(left, right, (((1,), (1,)), ((), ())), preferred_element_...  35.4 us
    all_to_all x3, waiting for transfers between devices, local(): lax.all_to_all(outgoing[:, start:start + step].reshape(owners, capacity,...  34.8 us
    dot_general x6, matrix products, matmul_tn(): lax.dot_general(left, right, (((0,), (0,)), ((), ())), preferred_element_...  29.8 us
  transfers between devices with their start and end apart: 64, of which 34 were waited for; matrix products, arithmetic and copies ran while one was open for 11% of the time, Pallas kernels for 0%

commit v1 on v0

--- a/solution.py
+++ b/solution.py
@@ -302,13 +302,21 @@
     pieces = []
     step = 256
     for start in range(0, width, step):
-        incoming = lax.all_to_all(
-            outgoing[:, start : start + step].reshape(owners, capacity, step),
-            "vocab",
-            split_axis=0,
-            concat_axis=0,
-            tiled=True,
-        )
+        array = outgoing[:, start : start + step].reshape(owners, capacity, step)
+        ways, here = (lax.axis_size("vocab"), lax.axis_index("vocab"))
+        width_2 = array.shape[0] // ways
+        lengths_2 = list(array.shape)
+        lengths_2[0] = width_2
+        height = lengths_2[0]
+        lengths_2[0] = height * ways
+        incoming = jnp.zeros(lengths_2, array.dtype)
+        for mask in range(ways):
+            part = lax.dynamic_slice_in_dim(array, (here ^ mask) * width_2, width_2, axis=0)
+            if mask:
+                part = lax.ppermute(part, "vocab", [(d, d ^ mask) for d in range(ways)])
+            incoming = lax.dynamic_update_slice_in_dim(
+                incoming, part, (here ^ mask) * height, axis=0
+            )
         dense = matmul(hits, incoming.reshape(owners * capacity, step)).astype(bf)
         pieces.append(sum_over_dp(dense))
     grad_word = jnp.concatenate(pieces, 1)

time: 790 us -> 755 us (0.956)
  waiting for transfers between devices: 292 us -> 247 us
  starting transfers between devices: 82.7 us -> 109 us
  local copies, waits for them, and re-layouts: 108 us -> 98.6 us
    ppermute x51, waiting for transfers between devices: 176 us -> 123 us  [swap(): return lax.ppermute(value, axis_name, [(i, i ^ bit) for i in range(size)])]
    ppermute x0 -> x21, waiting for transfers between devices: none -> 42.1 us  [local(): part = lax.ppermute(part, 'vocab', [(d, d ^ mask) for d in range(ways)])]
    all_to_all x3 -> x0, waiting for transfers between devices: 34.8 us -> none  [local(): lax.all_to_all(outgoing[:, start:start + step].reshape(owners, capacity,...]
    ppermute x0 -> x21, starting transfers between devices: none -> 31.1 us  [local(): part = lax.ppermute(part, 'vocab', [(d, d ^ mask) for d in range(ways)])]
    all_to_all x3 -> x0, starting transfers between devices: 13.1 us -> none  [local(): lax.all_to_all(outgoing[:, start:start + step].reshape(owners, capacity,...]
    ppermute x51, starting transfers between devices: 50.7 us -> 59 us  [swap(): return lax.ppermute(value, axis_name, [(i, i ^ bit) for i in range(size)])]
  transfers between devices with their start and end apart: 64 -> 82, of which waited for: 34 -> 48; matrix products, arithmetic and copies ran while one was open for 11% -> 8% of each run, Pallas kernels for 0% -> 0%
where the time goes in v1:
time: 755 us; the launch traced here: 751 us
  waiting for transfers between devices  247 us (33%)
  matrix products  196 us (26%)
  starting transfers between devices  109 us (14%)
  local copies, waits for them, and re-layouts  98.6 us (13%)
  other arithmetic  83.4 us (11%)
  blocking collectives  11.7 us (2%)
    ppermute x51, waiting for transfers between devices, swap(): return lax.ppermute(value, axis_name, [(i, i ^ bit) for i in range(size)])  123 us
    dot_general x10, matrix products, matmul(): return jnp.dot(left, right, preferred_element_type=jnp.float32)  72.6 us
    all_to_all x1, waiting for transfers between devices, local(): lax.all_to_all(found, 'vocab', split_axis=0, concat_axis=0, tiled=True)  69.1 us
    ppermute x51, starting transfers between devices, swap(): return lax.ppermute(value, axis_name, [(i, i ^ bit) for i in range(size)])  59 us
    ppermute x21, waiting for transfers between devices, local(): part = lax.ppermute(part, 'vocab', [(d, d ^ mask) for d in range(ways)])  42.1 us
    dot_general x6, matrix products, matmul_nt(): lax.dot_general(left, right, (((1,), (1,)), ((), ())), preferred_element_...  35.2 us
    dot_general x6, matrix products, matmul_tn(): lax.dot_general(left, right, (((0,), (0,)), ((), ())), preferred_element_...  31.8 us
    ppermute x21, starting transfers between devices, local(): part = lax.ppermute(part, 'vocab', [(d, d ^ mask) for d in range(ways)])  31.1 us
  transfers between devices with their start and end apart: 82, of which 48 were waited for; matrix products, arithmetic and copies ran while one was open for 8% of the time, Pallas kernels for 0%

profile of v1, /device:TPU:0, one launch (start us, length us, event | category | flops | bytes accessed | tf_op | source)
XLA Modules:
  0.0 750.7 jit_solution(13133345940846752176)
XLA Ops:
  7.8 4.3 scatter_custom_fusion
  12.1 11.7 %all_to_all.14 = s32[8,1,256]{2,1,0:T(1,128)S(1)} all-to-all(s32[8,1,256]{2,1,0:T(1,128)S(1)} %bitcast.734), channel_id=1, replica_groups=mesh['dp'=4,'vocab'=8] {'vocab'}, dimensions={0} | all-to-all | bytes 16384 | tf_op jit(solution)/shard_map/all_to_all | solution.py:208
  23.9 13.5 %gather_fusion = bf16[2048,768]{1,0:T(8,128)(2,1)} fusion(bf16[3840,768]{1,0:T(8,128)(2,1)} %param.31, s32[2048]{0:T(1024)S(1)} %broadcast_clamp_fusion), kind=kCustom, calls=%fused_computation | custom fusion | bytes 6299648 | tf_op jit(solution)/shard_map/gather | solution.py:210
  37.4 3.3 broadcast_select_fusion
  40.7 5.1 all-to-all-start.1
  48.2 69.1 %all-to-all-done.1 = bf16[8,256,768]{2,1,0:T(8,128)(2,1)} async-done(((bf16[8,256,768]{2,1,0:T(8,128)(2,1)}), bf16[8,256,768]{2,1,0:T(8,128)(2,1)}, u32[]{:S(2)}, u32[]{:S(2)}) %all-to-all-start.1) | async-done | bytes 3145760 | tf_op jit(solution)/shard_map/all_to_all | solution.py:212
  117.3 8.0 %gather_fusion.1 = bf16[1024,768]{1,0:T(8,128)(2,1)} fusion(bf16[2048,768]{1,0:T(8,128)(2,1)} %bitcast.25, s32[1024]{0:T(1024)S(1)} %broadcast_clamp_fusion.1), kind=kCustom, calls=%fused_computation.1 | custom fusion | bytes 3149824 | tf_op jit(solution)/shard_map/gather | solution.py:213
  157.3 3.9 reshape.625
  164.1 25.6 %while.26 = (s32[]{:T(128)}, bf16[2,512,12,64]{1,3,2,0:T(8,128)(2,1)}, f32[2,12,512,1]{2,1,3,0:T(8,128)}, bf16[2,512,12,64]{1,3,2,0:T(8,128)(2,1)}, s32[2]{0:T(1...) while((s32[]{:T(128)}, ...), condition=%wide.region_9.10_spmd, body=%wide.region_6.9_spmd.sunk | while | flops 843442688 | bytes 47411840 | solution.py:236
  165.5 4.1 fusion.269
  172.8 4.1 fusion.271
  178.2 4.1 fusion.269
  185.5 4.2 fusion.271
  189.7 3.6 copy.214
  198.2 35.1 %multiply_convert_fusion.1 = (bf16[1024,3072]{1,0:T(8,128)(2,1)S(1)}, f32[1024,3072]{1,0:T(8,128)}, f32[1024,3072]{1,0:T(8,128)}) fusion(f32[3072]{0:T(1024)S(1)} %copy-done.75, bf16[768,3072]{1,0:T(8,128)(2,1)S(1)} %bitcast.744, f32[1024,768]{1,0:T(8,128)S(1)} %get-tuple-element.355, f32[768]{0:T(1024)S(1)} %copy-done.80, f32[768]{0:T(1024)S(1)} %copy-done.66, ...), kind=kOutput, calls=%fused_computation.69 | convolution fusion | flops 5043388416 | bytes 39348224 | tf_op jit(solution)/shard_map/dot_general | solution.py:20
  233.3 5.5 fusion.215
  245.0 7.7 %convolution_convert_fusion = bf16[3072,768]{1,0:T(8,128)(2,1)} fusion(bf16[1024,3072]{1,0:T(8,128)(2,1)S(1)} %get-tuple-element.250, f32[1024,768]{1,0:T(8,128)S(1)} %get-tuple-element.249, f32[1024]{0:T(1024)S(1)} %negate_multiply_fusion.3), kind=kOutput, calls=%fused_computation.92 | convolution fusion | flops 4835770368 | bytes 14159872 | tf_op jit(solution)/shard_map/dot_general | solution.py:24
  252.7 19.4 %fusion.216 = (bf16[3072]{0:T(1024)(128)(2,1)}, bf16[1024,3072]{1,0:T(8,128)(2,1)}) fusion(f32[1024,3072]{1,0:T(8,128)} %get-tuple-element.251, bf16[3072,768]{1,0:T(8,128)(2,1)} %param.47, f32[1024,768]{1,0:T(8,128)} %copy-done.19, f32[1024]{0:T(1024)S(1)} %negate_multiply_fusion.3, f32[1024,3072]{1,0:T(8,128)} %get-tuple-element.356, f32[3072]{0:T(1024)S(1)} %copy-done.75), kind=kOutput, calls=%fused_computation.532 | convolution fusion | flops 4883739648 | bytes 39344128 | tf_op jit(solution)/shard_map/dot_general | solution.py:30
  272.1 10.7 %convolution_convert_fusion.1 = bf16[768,3072]{1,0:T(8,128)(2,1)} fusion(bf16[1024,3072]{1,0:T(8,128)(2,1)} %get-tuple-element.361, f32[1024,768]{1,0:T(8,128)} %copy-done.17, f32[768]{0:T(1024)S(1)} %copy-done.80, f32[768]{0:T(1024)S(1)} %copy-done.66, f32[1024]{0:T(1024)S(1)} %fusion.191, f32[1024]{0:T(1024)S(1)} %broadcast_multiply_fusion.1), kind=kOutput, calls=%fused_computation.93 | convolution fusion | flops 4838129664 | bytes 14170112 | tf_op jit(solution)/shard_map/dot_general | solution.py:24
  282.9 8.9 %multiply_reduce_fusion.2 = (bf16[768]{0:T(1024)(128)(2,1)}, f32[1024]{0:T(1024)S(1)}, bf16[768]{0:T(1024)(128)(2,1)}, f32[1024,768]{1,0:T(8,128)S(1)}) fusion(f32[1024,768]{1,0:T(8,128)S(1)} %copy-done.18, f32[1024]{0:T(1024)S(1)} %fusion.191, f32[1024]{0:T(1024)S(1)} %broadcast_multiply_fusion.1, f32[768]{0:T(1024)S(1)} %copy-done.66, ...), kind=kOutput, calls=%fused_computation.116 | convolution fusion | flops 4839699456 | bytes 20469760 | tf_op jit(solution)/shard_map/dot_general | solution.py:30
  298.4 4.0 reshape.628
  305.3 56.1 %while.27 = (s32[]{:T(128)}, f32[2,512,12,64]{1,3,2,0:T(8,128)}, bf16[2,512,12,64]{1,3,2,0:T(8,128)(2,1)}, f32[2,512,12,64]{1,3,2,0:T(8,128)}, bf16[2,512,12,64]...) while((s32[]{:T(128)}, f32[2,512,12,64]{1,3,2,0:T(8,128)}, ...), condition=%wide.region_20.21_spmd, body=%wide.region_18.20_spmd.sunk | while | flops 2061232640 | bytes 161414480 | solution.py:264
  305.5 3.1 fusion.280
  309.9 7.3 multiply_reduce_fusion.9
  317.2 7.4 multiply_convert_fusion.3
  329.3 3.9 bitcast_dynamic-update-slice_fusion.11
  333.2 3.1 fusion.280
  337.6 7.3 multiply_reduce_fusion.9
  345.0 7.4 multiply_convert_fusion.3
  357.0 4.0 bitcast_dynamic-update-slice_fusion.11
  361.4 5.5 fusion.203
  385.2 3.3 fusion.113
  392.7 4.0 fusion.100
  407.1 4.4 fusion.103
  412.0 3.3 pad_maximum_fusion
  416.7 4.1 fusion.68
  423.7 5.9 collective-permute-done.1
  436.5 7.3 collective-permute-done.4
  444.8 3.5 collective-permute-start.16
  450.0 6.0 fusion.60
  461.1 9.9 %collective-permute-done.18 = bf16[1,256,256]{2,1,0:T(8,128)(2,1)S(1)} collective-permute-done((bf16[1,256,256]{2,1,0:T(8,128)(2,1)S(1)}, bf16[1,256,256]{2,1,0:T(8,128)(2,1)S(1)}, u32[]{:S(2)}, u32[]{:S(2)}) %collective-permute-start.18) | collective-permute-done | bytes 131104 | tf_op jit(solution)/shard_map/ppermute | solution.py:316
  473.9 6.2 collective-permute-start.31
  482.5 6.0 fusion.61
  493.3 10.0 %collective-permute-done.33 = bf16[1,256,256]{2,1,0:T(8,128)(2,1)S(1)} collective-permute-done((bf16[1,256,256]{2,1,0:T(8,128)(2,1)S(1)}, bf16[1,256,256]{2,1,0:T(8,128)(2,1)S(1)}, u32[]{:S(2)}, u32[]{:S(2)}) %collective-permute-start.33) | collective-permute-done | bytes 131104 | tf_op jit(solution)/shard_map/ppermute | solution.py:316
  512.4 6.4 fusion.62
  521.7 8.1 %collective-permute-done.26 = bf16[2,480,256]{2,1,0:T(8,128)(2,1)S(1)} collective-permute-done((bf16[2,480,256]{2,1,0:T(8,128)(2,1)S(1)}, bf16[2,480,256]{2,1,0:T(8,128)(2,1)S(1)}, u32[]{:S(2)}, u32[]{:S(2)}) %collective-permute-start.26) | collective-permute-done | bytes 491552 | tf_op jit(solution)/shard_map/ppermute | solution.py:76
  534.0 8.2 %collective-permute-done.41 = bf16[2,480,256]{2,1,0:T(8,128)(2,1)S(1)} collective-permute-done((bf16[2,480,256]{2,1,0:T(8,128)(2,1)S(1)}, bf16[2,480,256]{2,1,0:T(8,128)(2,1)S(1)}, u32[]{:S(2)}, u32[]{:S(2)}) %collective-permute-start.41) | collective-permute-done | bytes 491552 | tf_op jit(solution)/shard_map/ppermute | solution.py:76
  547.5 3.5 collective-permute-done.12
  561.8 3.4 collective-permute-done.38
  565.7 4.7 collective-permute-done.13
  572.6 3.1 collective-permute-done.28
  581.0 4.4 collective-permute-done.39
  590.8 8.7 %collective-permute-done.14 = bf16[2,480,256]{2,1,0:T(8,128)(2,1)S(1)} collective-permute-done((bf16[2,480,256]{2,1,0:T(8,128)(2,1)S(1)}, bf16[2,480,256]{2,1,0:T(8,128)(2,1)S(1)}, u32[]{:S(2)}, u32[]{:S(2)}) %collective-permute-start.14) | collective-permute-done | bytes 491552 | tf_op jit(solution)/shard_map/ppermute | solution.py:76
  601.3 11.1 %collective-permute-done.25 = bf16[2,480,256]{2,1,0:T(8,128)(2,1)S(1)} collective-permute-done((bf16[2,480,256]{2,1,0:T(8,128)(2,1)S(1)}, bf16[2,480,256]{2,1,0:T(8,128)(2,1)S(1)}, u32[]{:S(2)}, u32[]{:S(2)}) %collective-permute-start.25) | collective-permute-done | bytes 491552 | tf_op jit(solution)/shard_map/ppermute | solution.py:76
  616.8 6.4 collective-permute-done.40
  624.3 5.0 maximum_convert_fusion
  639.6 8.9 %collective-permute-done.72 = bf16[2,2,96,768]{3,2,0,1:T(8,128)(2,1)S(1)} collective-permute-done((bf16[2,2,96,768]{3,2,0,1:T(8,128)(2,1)S(1)}, bf16[2,2,96,768]{3,2,0,1:T(8,128)(2,1)S(1)}, u32[]{:S(2)}, u32[]{:S(2)}) %collective-permute-start.72) | collective-permute-done | bytes 589856 | tf_op jit(solution)/shard_map/ppermute | solution.py:76
  651.5 9.6 %collective-permute-done.60 = bf16[2,2,24,3072]{3,2,0,1:T(8,128)(2,1)S(1)} collective-permute-done((bf16[2,2,24,3072]{3,2,0,1:T(8,128)(2,1)S(1)}, bf16[2,2,24,3072]{3,2,0,1:T(8,128)(2,1)S(1)}, u32[]{:S(2)}, u32[]{:S(2)}) %collective-permute-start.60) | collective-permute-done | bytes 589856 | tf_op jit(solution)/shard_map/ppermute | solution.py:76
  668.2 3.2 collective-permute-done.59
  681.8 3.1 collective-permute-start.76
  701.4 7.8 %collective-permute-done.68 = bf16[24,1536]{1,0:T(8,128)(2,1)S(1)} collective-permute-done((bf16[24,1536]{1,0:T(8,128)(2,1)S(1)}, bf16[24,1536]{1,0:T(8,128)(2,1)S(1)}, u32[]{:S(2)}, u32[]{:S(2)}) %collective-permute-start.68) | collective-permute-done | bytes 73760 | tf_op jit(solution)/shard_map/ppermute | solution.py:76
  713.7 5.4 collective-permute-done.49
  726.0 3.1 collective-permute-done.50
  729.1 4.2 collective-permute-done.51
  (632 shorter events, 274.9 us)
Async XLA Ops:
  40.7 76.6 %all-to-all-start.1 = ((bf16[8,256,768]{2,1,0:T(8,128)(2,1)}), bf16[8,256,768]{2,1,0:T(8,128)(2,1)}, u32[]{:S(2)}, u32[]{:S(2)}) async-start(bf16[8,256,768]{2,1,0:T(8,128)(2,1)} %broadcast_select_fusion), calls=%async_computation.1 | async-start | bytes 6291456 | tf_op jit(solution)/shard_map/all_to_all | solution.py:212
  403.3 226.0 %collective-permute-start.69 = (bf16[4,384,768]{2,1,0:T(8,128)(2,1)}, bf16[4,384,768]{2,1,0:T(8,128)(2,1)}, u32[]{:S(2)}, u32[]{:S(2)}) collective-permute-start(bf16[4,384,768]{2,1,0:T(8,128)(2,1)} %dynamic-slice_bitcast_fusion.2), channel_id=1, source_target_pairs={{0,1},{1,0},{2,3},{3,2},{4,5},{5,4},{6,7},{7,6},{8,9},{9,8},{10,11... | collective-permute-start | bytes 7077896 | tf_op jit(solution)/shard_map/ppermute | solution.py:76
  405.0 229.9 %collective-permute-start.57 = (bf16[4,96,3072]{2,1,0:T(8,128)(2,1)}, bf16[4,96,3072]{2,1,0:T(8,128)(2,1)}, u32[]{:S(2)}, u32[]{:S(2)}) collective-permute-start(bf16[4,96,3072]{2,1,0:T(8,128)(2,1)} %dynamic-slice_bitcast_fusion.3), channel_id=1, source_target_pairs={{0,1},{1,0},{2,3},{3,2},{4,5},{5,4},{6,7},{7,6},{8,9},{9,8},{10,11... | collective-permute-start | bytes 7077896 | tf_op jit(solution)/shard_map/ppermute | solution.py:76
  421.4 8.3 %collective-permute-start.1 = (bf16[1,256,256]{2,1,0:T(8,128)(2,1)S(1)}, bf16[1,256,256]{2,1,0:T(8,128)(2,1)S(1)}, u32[]{:S(2)}, u32[]{:S(2)}) collective-permute-start(bf16[1,256,256]{2,1,0:T(8,128)(2,1)S(1)} %get-tuple-element.300), channel_id=1, source_target_pairs={{0,2},{1,3},{2,0},{3,1},{4,6},{5,7},{6,4},{7,5},{8,10},{9,11},{10,... | collective-permute-start | bytes 393224 | tf_op jit(solution)/shard_map/ppermute | solution.py:316
  421.4 10.3 %collective-permute-start.2 = (bf16[1,256,256]{2,1,0:T(8,128)(2,1)S(1)}, bf16[1,256,256]{2,1,0:T(8,128)(2,1)S(1)}, u32[]{:S(2)}, u32[]{:S(2)}) collective-permute-start(bf16[1,256,256]{2,1,0:T(8,128)(2,1)S(1)} %get-tuple-element.299), channel_id=1, source_target_pairs={{0,3},{1,2},{2,1},{3,0},{4,7},{5,6},{6,5},{7,4},{8,11},{9,10},{10,... | collective-permute-start | bytes 393224 | tf_op jit(solution)/shard_map/ppermute | solution.py:316
  423.6 12.9 %collective-permute-start.3 = (bf16[1,256,256]{2,1,0:T(8,128)(2,1)S(1)}, bf16[1,256,256]{2,1,0:T(8,128)(2,1)S(1)}, u32[]{:S(2)}, u32[]{:S(2)}) collective-permute-start(bf16[1,256,256]{2,1,0:T(8,128)(2,1)S(1)} %get-tuple-element.298), channel_id=1, source_target_pairs={{0,4},{1,5},{2,6},{3,7},{4,0},{5,1},{6,2},{7,3},{8,12},{9,13},{10,... | collective-permute-start | bytes 393224 | tf_op jit(solution)/shard_map/ppermute | solution.py:316
  429.6 14.2 %collective-permute-start.4 = (bf16[1,256,256]{2,1,0:T(8,128)(2,1)S(1)}, bf16[1,256,256]{2,1,0:T(8,128)(2,1)S(1)}, u32[]{:S(2)}, u32[]{:S(2)}) collective-permute-start(bf16[1,256,256]{2,1,0:T(8,128)(2,1)S(1)} %get-tuple-element.297), channel_id=1, source_target_pairs={{0,5},{1,4},{2,7},{3,6},{4,1},{5,0},{6,3},{7,2},{8,13},{9,12},{10,... | collective-permute-start | bytes 393224 | tf_op jit(solution)/shard_map/ppermute | solution.py:316
  431.7 13.0 %collective-permute-start.5 = (bf16[1,256,256]{2,1,0:T(8,128)(2,1)S(1)}, bf16[1,256,256]{2,1,0:T(8,128)(2,1)S(1)}, u32[]{:S(2)}, u32[]{:S(2)}) collective-permute-start(bf16[1,256,256]{2,1,0:T(8,128)(2,1)S(1)} %get-tuple-element.296), channel_id=1, source_target_pairs={{0,6},{1,7},{2,4},{3,5},{4,2},{5,3},{6,0},{7,1},{8,14},{9,15},{10,... | collective-permute-start | bytes 393224 | tf_op jit(solution)/shard_map/ppermute | solution.py:316
  436.5 11.8 %collective-permute-start.6 = (bf16[1,256,256]{2,1,0:T(8,128)(2,1)S(1)}, bf16[1,256,256]{2,1,0:T(8,128)(2,1)S(1)}, u32[]{:S(2)}, u32[]{:S(2)}) collective-permute-start(bf16[1,256,256]{2,1,0:T(8,128)(2,1)S(1)} %get-tuple-element.295), channel_id=1, source_target_pairs={{0,7},{1,6},{2,5},{3,4},{4,3},{5,2},{6,1},{7,0},{8,15},{9,14},{10,... | collective-permute-start | bytes 393224 | tf_op jit(solution)/shard_map/ppermute | solution.py:316
  443.8 12.4 %collective-permute-start.15 = (bf16[1,256,256]{2,1,0:T(8,128)(2,1)S(1)}, bf16[1,256,256]{2,1,0:T(8,128)(2,1)S(1)}, u32[]{:S(2)}, u32[]{:S(2)}) collective-permute-start(bf16[1,256,256]{2,1,0:T(8,128)(2,1)S(1)} %get-tuple-element.309), channel_id=1, source_target_pairs={{0,1},{1,0},{2,3},{3,2},{4,5},{5,4},{6,7},{7,6},{8,9},{9,8},{10,11... | collective-permute-start | bytes 393224 | tf_op jit(solution)/shard_map/ppermute | solution.py:316
  444.8 12.3 %collective-permute-start.16 = (bf16[1,256,256]{2,1,0:T(8,128)(2,1)S(1)}, bf16[1,256,256]{2,1,0:T(8,128)(2,1)S(1)}, u32[]{:S(2)}, u32[]{:S(2)}) collective-permute-start(bf16[1,256,256]{2,1,0:T(8,128)(2,1)S(1)} %get-tuple-element.308), channel_id=1, source_target_pairs={{0,2},{1,3},{2,0},{3,1},{4,6},{5,7},{6,4},{7,5},{8,10},{9,11},{10,... | collective-permute-start | bytes 393224 | tf_op jit(solution)/shard_map/ppermute | solution.py:316
  448.3 10.4 %collective-permute-start.17 = (bf16[1,256,256]{2,1,0:T(8,128)(2,1)S(1)}, bf16[1,256,256]{2,1,0:T(8,128)(2,1)S(1)}, u32[]{:S(2)}, u32[]{:S(2)}) collective-permute-start(bf16[1,256,256]{2,1,0:T(8,128)(2,1)S(1)} %get-tuple-element.307), channel_id=1, source_target_pairs={{0,3},{1,2},{2,1},{3,0},{4,7},{5,6},{6,5},{7,4},{8,11},{9,10},{10,... | collective-permute-start | bytes 393224 | tf_op jit(solution)/shard_map/ppermute | solution.py:316
  456.2 14.9 %collective-permute-start.18 = (bf16[1,256,256]{2,1,0:T(8,128)(2,1)S(1)}, bf16[1,256,256]{2,1,0:T(8,128)(2,1)S(1)}, u32[]{:S(2)}, u32[]{:S(2)}) collective-permute-start(bf16[1,256,256]{2,1,0:T(8,128)(2,1)S(1)} %get-tuple-element.306), channel_id=1, source_target_pairs={{0,4},{1,5},{2,6},{3,7},{4,0},{5,1},{6,2},{7,3},{8,12},{9,13},{10,... | collective-permute-start | bytes 393224 | tf_op jit(solution)/shard_map/ppermute | solution.py:316
  457.1 16.6 %collective-permute-start.19 = (bf16[1,256,256]{2,1,0:T(8,128)(2,1)S(1)}, bf16[1,256,256]{2,1,0:T(8,128)(2,1)S(1)}, u32[]{:S(2)}, u32[]{:S(2)}) collective-permute-start(bf16[1,256,256]{2,1,0:T(8,128)(2,1)S(1)} %get-tuple-element.305), channel_id=1, source_target_pairs={{0,5},{1,4},{2,7},{3,6},{4,1},{5,0},{6,3},{7,2},{8,13},{9,12},{10,... | collective-permute-start | bytes 393224 | tf_op jit(solution)/shard_map/ppermute | solution.py:316
  458.8 15.1 %collective-permute-start.20 = (bf16[1,256,256]{2,1,0:T(8,128)(2,1)S(1)}, bf16[1,256,256]{2,1,0:T(8,128)(2,1)S(1)}, u32[]{:S(2)}, u32[]{:S(2)}) collective-permute-start(bf16[1,256,256]{2,1,0:T(8,128)(2,1)S(1)} %get-tuple-element.304), channel_id=1, source_target_pairs={{0,6},{1,7},{2,4},{3,5},{4,2},{5,3},{6,0},{7,1},{8,14},{9,15},{10,... | collective-permute-start | bytes 393224 | tf_op jit(solution)/shard_map/ppermute | solution.py:316
  471.1 9.0 %collective-permute-start.21 = (bf16[1,256,256]{2,1,0:T(8,128)(2,1)S(1)}, bf16[1,256,256]{2,1,0:T(8,128)(2,1)S(1)}, u32[]{:S(2)}, u32[]{:S(2)}) collective-permute-start(bf16[1,256,256]{2,1,0:T(8,128)(2,1)S(1)} %get-tuple-element.303), channel_id=1, source_target_pairs={{0,7},{1,6},{2,5},{3,4},{4,3},{5,2},{6,1},{7,0},{8,15},{9,14},{10,... | collective-permute-start | bytes 393224 | tf_op jit(solution)/shard_map/ppermute | solution.py:316
  473.7 14.9 %collective-permute-start.30 = (bf16[1,256,256]{2,1,0:T(8,128)(2,1)S(1)}, bf16[1,256,256]{2,1,0:T(8,128)(2,1)S(1)}, u32[]{:S(2)}, u32[]{:S(2)}) collective-permute-start(bf16[1,256,256]{2,1,0:T(8,128)(2,1)S(1)} %get-tuple-element.317), channel_id=1, source_target_pairs={{0,1},{1,0},{2,3},{3,2},{4,5},{5,4},{6,7},{7,6},{8,9},{9,8},{10,11... | collective-permute-start | bytes 393224 | tf_op jit(solution)/shard_map/ppermute | solution.py:316
  473.9 15.4 %collective-permute-start.31 = (bf16[1,256,256]{2,1,0:T(8,128)(2,1)S(1)}, bf16[1,256,256]{2,1,0:T(8,128)(2,1)S(1)}, u32[]{:S(2)}, u32[]{:S(2)}) collective-permute-start(bf16[1,256,256]{2,1,0:T(8,128)(2,1)S(1)} %get-tuple-element.316), channel_id=1, source_target_pairs={{0,2},{1,3},{2,0},{3,1},{4,6},{5,7},{6,4},{7,5},{8,10},{9,11},{10,... | collective-permute-start | bytes 393224 | tf_op jit(solution)/shard_map/ppermute | solution.py:316
  480.1 11.4 %collective-permute-start.32 = (bf16[1,256,256]{2,1,0:T(8,128)(2,1)S(1)}, bf16[1,256,256]{2,1,0:T(8,128)(2,1)S(1)}, u32[]{:S(2)}, u32[]{:S(2)}) collective-permute-start(bf16[1,256,256]{2,1,0:T(8,128)(2,1)S(1)} %get-tuple-element.315), channel_id=1, source_target_pairs={{0,3},{1,2},{2,1},{3,0},{4,7},{5,6},{6,5},{7,4},{8,11},{9,10},{10,... | collective-permute-start | bytes 393224 | tf_op jit(solution)/shard_map/ppermute | solution.py:316
  488.7 14.7 %collective-permute-start.33 = (bf16[1,256,256]{2,1,0:T(8,128)(2,1)S(1)}, bf16[1,256,256]{2,1,0:T(8,128)(2,1)S(1)}, u32[]{:S(2)}, u32[]{:S(2)}) collective-permute-start(bf16[1,256,256]{2,1,0:T(8,128)(2,1)S(1)} %get-tuple-element.314), channel_id=1, source_target_pairs={{0,4},{1,5},{2,6},{3,7},{4,0},{5,1},{6,2},{7,3},{8,12},{9,13},{10,... | collective-permute-start | bytes 393224 | tf_op jit(solution)/shard_map/ppermute | solution.py:316
  489.3 16.8 %collective-permute-start.34 = (bf16[1,256,256]{2,1,0:T(8,128)(2,1)S(1)}, bf16[1,256,256]{2,1,0:T(8,128)(2,1)S(1)}, u32[]{:S(2)}, u32[]{:S(2)}) collective-permute-start(bf16[1,256,256]{2,1,0:T(8,128)(2,1)S(1)} %get-tuple-element.313), channel_id=1, source_target_pairs={{0,5},{1,4},{2,7},{3,6},{4,1},{5,0},{6,3},{7,2},{8,13},{9,12},{10,... | collective-permute-start | bytes 393224 | tf_op jit(solution)/shard_map/ppermute | solution.py:316
  491.5 16.1 %collective-permute-start.35 = (bf16[1,256,256]{2,1,0:T(8,128)(2,1)S(1)}, bf16[1,256,256]{2,1,0:T(8,128)(2,1)S(1)}, u32[]{:S(2)}, u32[]{:S(2)}) collective-permute-start(bf16[1,256,256]{2,1,0:T(8,128)(2,1)S(1)} %get-tuple-element.312), channel_id=1, source_target_pairs={{0,6},{1,7},{2,4},{3,5},{4,2},{5,3},{6,0},{7,1},{8,14},{9,15},{10,... | collective-permute-start | bytes 393224 | tf_op jit(solution)/shard_map/ppermute | solution.py:316
  506.0 14.1 %collective-permute-start.11 = (bf16[2,480,256]{2,1,0:T(8,128)(2,1)S(1)}, bf16[2,480,256]{2,1,0:T(8,128)(2,1)S(1)}, u32[]{:S(2)}, u32[]{:S(2)}) collective-permute-start(bf16[2,480,256]{2,1,0:T(8,128)(2,1)S(1)} %dynamic-slice_bitcast_fusion.9), channel_id=1, source_target_pairs={{0,16},{8,24},{16,0},{24,8},{1,17},{9,25},{17,1},{25,9},{2,18},{10... | collective-permute-start | bytes 1474568 | tf_op jit(solution)/shard_map/ppermute | solution.py:76
  507.6 23.8 %collective-permute-start.7 = (bf16[2,480,256]{2,1,0:T(8,128)(2,1)S(1)}, bf16[2,480,256]{2,1,0:T(8,128)(2,1)S(1)}, u32[]{:S(2)}, u32[]{:S(2)}) collective-permute-start(bf16[2,480,256]{2,1,0:T(8,128)(2,1)S(1)} %dynamic-slice_bitcast_fusion.10), channel_id=1, source_target_pairs={{0,8},{8,0},{16,24},{24,16},{1,9},{9,1},{17,25},{25,17},{2,10},{10... | collective-permute-start | bytes 1474568 | tf_op jit(solution)/shard_map/ppermute | solution.py:76
  510.8 19.0 %collective-permute-start.26 = (bf16[2,480,256]{2,1,0:T(8,128)(2,1)S(1)}, bf16[2,480,256]{2,1,0:T(8,128)(2,1)S(1)}, u32[]{:S(2)}, u32[]{:S(2)}) collective-permute-start(bf16[2,480,256]{2,1,0:T(8,128)(2,1)S(1)} %dynamic-slice_bitcast_fusion.7), channel_id=1, source_target_pairs={{0,16},{8,24},{16,0},{24,8},{1,17},{9,25},{17,1},{25,9},{2,18},{10... | collective-permute-start | bytes 1474568 | tf_op jit(solution)/shard_map/ppermute | solution.py:76
  520.1 13.2 %collective-permute-start.22 = (bf16[2,480,256]{2,1,0:T(8,128)(2,1)S(1)}, bf16[2,480,256]{2,1,0:T(8,128)(2,1)S(1)}, u32[]{:S(2)}, u32[]{:S(2)}) collective-permute-start(bf16[2,480,256]{2,1,0:T(8,128)(2,1)S(1)} %dynamic-slice_bitcast_fusion.8), channel_id=1, source_target_pairs={{0,8},{8,0},{16,24},{24,16},{1,9},{9,1},{17,25},{25,17},{2,10},{10... | collective-permute-start | bytes 1474568 | tf_op jit(solution)/shard_map/ppermute | solution.py:76
  529.8 12.4 %collective-permute-start.41 = (bf16[2,480,256]{2,1,0:T(8,128)(2,1)S(1)}, bf16[2,480,256]{2,1,0:T(8,128)(2,1)S(1)}, u32[]{:S(2)}, u32[]{:S(2)}) collective-permute-start(bf16[2,480,256]{2,1,0:T(8,128)(2,1)S(1)} %dynamic-slice_bitcast_fusion.5), channel_id=1, source_target_pairs={{0,16},{8,24},{16,0},{24,8},{1,17},{9,25},{17,1},{25,9},{2,18},{10... | collective-permute-start | bytes 1474568 | tf_op jit(solution)/shard_map/ppermute | solution.py:76
  531.5 14.2 %collective-permute-start.37 = (bf16[2,480,256]{2,1,0:T(8,128)(2,1)S(1)}, bf16[2,480,256]{2,1,0:T(8,128)(2,1)S(1)}, u32[]{:S(2)}, u32[]{:S(2)}) collective-permute-start(bf16[2,480,256]{2,1,0:T(8,128)(2,1)S(1)} %dynamic-slice_bitcast_fusion.6), channel_id=1, source_target_pairs={{0,8},{8,0},{16,24},{24,16},{1,9},{9,1},{17,25},{25,17},{2,10},{10... | collective-permute-start | bytes 1474568 | tf_op jit(solution)/shard_map/ppermute | solution.py:76
  533.3 17.7 %collective-permute-start.12 = (bf16[480,256]{1,0:T(8,128)(2,1)S(1)}, bf16[480,256]{1,0:T(8,128)(2,1)S(1)}, u32[]{:S(2)}, u32[]{:S(2)}) collective-permute-start(bf16[480,256]{1,0:T(8,128)(2,1)S(1)} %dynamic-slice_bitcast_fusion.21), channel_id=1, source_target_pairs={{0,8},{8,0},{16,24},{24,16},{1,9},{9,1},{17,25},{25,17},{2,10},{10... | collective-permute-start | bytes 737288 | tf_op jit(solution)/shard_map/ppermute | solution.py:76
  542.2 9.3 %collective-permute-start.8 = (bf16[480,256]{1,0:T(8,128)(2,1)S(1)}, bf16[480,256]{1,0:T(8,128)(2,1)S(1)}, u32[]{:S(2)}, u32[]{:S(2)}) collective-permute-start(bf16[480,256]{1,0:T(8,128)(2,1)S(1)} %dynamic-slice_bitcast_fusion.22), channel_id=1, source_target_pairs={{0,16},{8,24},{16,0},{24,8},{1,17},{9,25},{17,1},{25,9},{2,18},{10... | collective-permute-start | bytes 737288 | tf_op jit(solution)/shard_map/ppermute | solution.py:76
  545.7 10.5 %collective-permute-start.27 = (bf16[480,256]{1,0:T(8,128)(2,1)S(1)}, bf16[480,256]{1,0:T(8,128)(2,1)S(1)}, u32[]{:S(2)}, u32[]{:S(2)}) collective-permute-start(bf16[480,256]{1,0:T(8,128)(2,1)S(1)} %dynamic-slice_bitcast_fusion.19), channel_id=1, source_target_pairs={{0,8},{8,0},{16,24},{24,16},{1,9},{9,1},{17,25},{25,17},{2,10},{10... | collective-permute-start | bytes 737288 | tf_op jit(solution)/shard_map/ppermute | solution.py:76
  551.0 8.6 %collective-permute-start.23 = (bf16[480,256]{1,0:T(8,128)(2,1)S(1)}, bf16[480,256]{1,0:T(8,128)(2,1)S(1)}, u32[]{:S(2)}, u32[]{:S(2)}) collective-permute-start(bf16[480,256]{1,0:T(8,128)(2,1)S(1)} %dynamic-slice_bitcast_fusion.20), channel_id=1, source_target_pairs={{0,16},{8,24},{16,0},{24,8},{1,17},{9,25},{17,1},{25,9},{2,18},{10... | collective-permute-start | bytes 737288 | tf_op jit(solution)/shard_map/ppermute | solution.py:76
  551.6 8.6 %collective-permute-start.42 = (bf16[480,256]{1,0:T(8,128)(2,1)S(1)}, bf16[480,256]{1,0:T(8,128)(2,1)S(1)}, u32[]{:S(2)}, u32[]{:S(2)}) collective-permute-start(bf16[480,256]{1,0:T(8,128)(2,1)S(1)} %dynamic-slice_bitcast_fusion.17), channel_id=1, source_target_pairs={{0,8},{8,0},{16,24},{24,16},{1,9},{9,1},{17,25},{25,17},{2,10},{10... | collective-permute-start | bytes 737288 | tf_op jit(solution)/shard_map/ppermute | solution.py:76
  556.2 8.9 %collective-permute-start.38 = (bf16[480,256]{1,0:T(8,128)(2,1)S(1)}, bf16[480,256]{1,0:T(8,128)(2,1)S(1)}, u32[]{:S(2)}, u32[]{:S(2)}) collective-permute-start(bf16[480,256]{1,0:T(8,128)(2,1)S(1)} %dynamic-slice_bitcast_fusion.18), channel_id=1, source_target_pairs={{0,16},{8,24},{16,0},{24,8},{1,17},{9,25},{17,1},{25,9},{2,18},{10... | collective-permute-start | bytes 737288 | tf_op jit(solution)/shard_map/ppermute | solution.py:76
  559.6 10.9 %collective-permute-start.13 = (bf16[480,256]{1,0:T(8,128)(2,1)S(1)}, bf16[480,256]{1,0:T(8,128)(2,1)S(1)}, u32[]{:S(2)}, u32[]{:S(2)}) collective-permute-start(bf16[480,256]{1,0:T(8,128)(2,1)S(1)} %fusion.133), channel_id=1, source_target_pairs={{0,16},{8,24},{16,0},{24,8},{1,17},{9,25},{17,1},{25,9},{2,18},{10... | collective-permute-start | bytes 737288 | tf_op jit(solution)/shard_map/ppermute | solution.py:76
  560.1 11.8 %collective-permute-start.9 = (bf16[480,256]{1,0:T(8,128)(2,1)S(1)}, bf16[480,256]{1,0:T(8,128)(2,1)S(1)}, u32[]{:S(2)}, u32[]{:S(2)}) collective-permute-start(bf16[480,256]{1,0:T(8,128)(2,1)S(1)} %fusion.134), channel_id=1, source_target_pairs={{0,8},{8,0},{16,24},{24,16},{1,9},{9,1},{17,25},{25,17},{2,10},{10... | collective-permute-start | bytes 737288 | tf_op jit(solution)/shard_map/ppermute | solution.py:76
  565.1 10.5 %collective-permute-start.28 = (bf16[480,256]{1,0:T(8,128)(2,1)S(1)}, bf16[480,256]{1,0:T(8,128)(2,1)S(1)}, u32[]{:S(2)}, u32[]{:S(2)}) collective-permute-start(bf16[480,256]{1,0:T(8,128)(2,1)S(1)} %fusion.131), channel_id=1, source_target_pairs={{0,16},{8,24},{16,0},{24,8},{1,17},{9,25},{17,1},{25,9},{2,18},{10... | collective-permute-start | bytes 737288 | tf_op jit(solution)/shard_map/ppermute | solution.py:76
  570.4 8.2 %collective-permute-start.24 = (bf16[480,256]{1,0:T(8,128)(2,1)S(1)}, bf16[480,256]{1,0:T(8,128)(2,1)S(1)}, u32[]{:S(2)}, u32[]{:S(2)}) collective-permute-start(bf16[480,256]{1,0:T(8,128)(2,1)S(1)} %fusion.132), channel_id=1, source_target_pairs={{0,8},{8,0},{16,24},{24,16},{1,9},{9,1},{17,25},{25,17},{2,10},{10... | collective-permute-start | bytes 737288 | tf_op jit(solution)/shard_map/ppermute | solution.py:76
  572.0 9.0 %collective-permute-start.43 = (bf16[480,256]{1,0:T(8,128)(2,1)S(1)}, bf16[480,256]{1,0:T(8,128)(2,1)S(1)}, u32[]{:S(2)}, u32[]{:S(2)}) collective-permute-start(bf16[480,256]{1,0:T(8,128)(2,1)S(1)} %fusion.129), channel_id=1, source_target_pairs={{0,16},{8,24},{16,0},{24,8},{1,17},{9,25},{17,1},{25,9},{2,18},{10... | collective-permute-start | bytes 737288 | tf_op jit(solution)/shard_map/ppermute | solution.py:76
  575.7 13.1 %collective-permute-start.10 = (bf16[2,480,256]{2,1,0:T(8,128)(2,1)S(1)}, bf16[2,480,256]{2,1,0:T(8,128)(2,1)S(1)}, u32[]{:S(2)}, u32[]{:S(2)}) collective-permute-start(bf16[2,480,256]{2,1,0:T(8,128)(2,1)S(1)} %pad_maximum_fusion.4), channel_id=1, source_target_pairs={{0,16},{8,24},{16,0},{24,8},{1,17},{9,25},{17,1},{25,9},{2,18},{10... | collective-permute-start | bytes 1474568 | tf_op jit(solution)/shard_map/ppermute | solution.py:76
  580.9 83.2 %collective-permute-start.45 = (bf16[4,128,3072]{2,1,0:T(8,128)(2,1)S(1)}, bf16[4,128,3072]{2,1,0:T(8,128)(2,1)S(1)}, u32[]{:S(2)}, u32[]{:S(2)}) collective-permute-start(bf16[4,128,3072]{2,1,0:T(8,128)(2,1)S(1)} %dynamic-slice_bitcast_fusion.1), channel_id=1, source_target_pairs={{0,1},{1,0},{2,3},{3,2},{4,5},{5,4},{6,7},{7,6},{8,9},{9,8},{10,11... | collective-permute-start | bytes 9437192 | tf_op jit(solution)/shard_map/ppermute | solution.py:76
  585.4 14.2 %collective-permute-start.14 = (bf16[2,480,256]{2,1,0:T(8,128)(2,1)S(1)}, bf16[2,480,256]{2,1,0:T(8,128)(2,1)S(1)}, u32[]{:S(2)}, u32[]{:S(2)}) collective-permute-start(bf16[2,480,256]{2,1,0:T(8,128)(2,1)S(1)} %pad_maximum_fusion.5), channel_id=1, source_target_pairs={{0,8},{8,0},{16,24},{24,16},{1,9},{9,1},{17,25},{25,17},{2,10},{10... | collective-permute-start | bytes 1474568 | tf_op jit(solution)/shard_map/ppermute | solution.py:76
  588.8 25.5 %collective-permute-start.29 = (bf16[2,480,256]{2,1,0:T(8,128)(2,1)S(1)}, bf16[2,480,256]{2,1,0:T(8,128)(2,1)S(1)}, u32[]{:S(2)}, u32[]{:S(2)}) collective-permute-start(bf16[2,480,256]{2,1,0:T(8,128)(2,1)S(1)} %pad_maximum_fusion.7), channel_id=1, source_target_pairs={{0,8},{8,0},{16,24},{24,16},{1,9},{9,1},{17,25},{25,17},{2,10},{10... | collective-permute-start | bytes 1474568 | tf_op jit(solution)/shard_map/ppermute | solution.py:76
  599.5 12.8 %collective-permute-start.25 = (bf16[2,480,256]{2,1,0:T(8,128)(2,1)S(1)}, bf16[2,480,256]{2,1,0:T(8,128)(2,1)S(1)}, u32[]{:S(2)}, u32[]{:S(2)}) collective-permute-start(bf16[2,480,256]{2,1,0:T(8,128)(2,1)S(1)} %pad_maximum_fusion.6), channel_id=1, source_target_pairs={{0,16},{8,24},{16,0},{24,8},{1,17},{9,25},{17,1},{25,9},{2,18},{10... | collective-permute-start | bytes 1474568 | tf_op jit(solution)/shard_map/ppermute | solution.py:76
  612.3 11.4 %collective-permute-start.44 = (bf16[2,480,256]{2,1,0:T(8,128)(2,1)S(1)}, bf16[2,480,256]{2,1,0:T(8,128)(2,1)S(1)}, u32[]{:S(2)}, u32[]{:S(2)}) collective-permute-start(bf16[2,480,256]{2,1,0:T(8,128)(2,1)S(1)} %pad_maximum_fusion.9), channel_id=1, source_target_pairs={{0,8},{8,0},{16,24},{24,16},{1,9},{9,1},{17,25},{25,17},{2,10},{10... | collective-permute-start | bytes 1474568 | tf_op jit(solution)/shard_map/ppermute | solution.py:76
  614.3 8.9 %collective-permute-start.40 = (bf16[2,480,256]{2,1,0:T(8,128)(2,1)S(1)}, bf16[2,480,256]{2,1,0:T(8,128)(2,1)S(1)}, u32[]{:S(2)}, u32[]{:S(2)}) collective-permute-start(bf16[2,480,256]{2,1,0:T(8,128)(2,1)S(1)} %pad_maximum_fusion.8), channel_id=1, source_target_pairs={{0,16},{8,24},{16,0},{24,8},{1,17},{9,25},{17,1},{25,9},{2,18},{10... | collective-permute-start | bytes 1474568 | tf_op jit(solution)/shard_map/ppermute | solution.py:76
  632.2 16.3 %collective-permute-start.72 = (bf16[2,2,96,768]{3,2,0,1:T(8,128)(2,1)S(1)}, bf16[2,2,96,768]{3,2,0,1:T(8,128)(2,1)S(1)}, u32[]{:S(2)}, u32[]{:S(2)}) collective-permute-start(bf16[2,2,96,768]{3,2,0,1:T(8,128)(2,1)S(1)} %bitcast.721), channel_id=1, source_target_pairs={{0,16},{8,24},{16,0},{24,8},{1,17},{9,25},{17,1},{25,9},{2,18},{10... | collective-permute-start | bytes 1769480 | tf_op jit(solution)/shard_map/ppermute | solution.py:76
  634.3 16.3 %collective-permute-start.70 = (bf16[2,2,96,768]{3,2,0,1:T(8,128)(2,1)S(1)}, bf16[2,2,96,768]{3,2,0,1:T(8,128)(2,1)S(1)}, u32[]{:S(2)}, u32[]{:S(2)}) collective-permute-start(bf16[2,2,96,768]{3,2,0,1:T(8,128)(2,1)S(1)} %bitcast.720), channel_id=1, source_target_pairs={{0,8},{8,0},{16,24},{24,16},{1,9},{9,1},{17,25},{25,17},{2,10},{10... | collective-permute-start | bytes 1769480 | tf_op jit(solution)/shard_map/ppermute | solution.py:76
  637.8 23.3 %collective-permute-start.60 = (bf16[2,2,24,3072]{3,2,0,1:T(8,128)(2,1)S(1)}, bf16[2,2,24,3072]{3,2,0,1:T(8,128)(2,1)S(1)}, u32[]{:S(2)}, u32[]{:S(2)}) collective-permute-start(bf16[2,2,24,3072]{3,2,0,1:T(8,128)(2,1)S(1)} %bitcast.723), channel_id=1, source_target_pairs={{0,16},{8,24},{16,0},{24,8},{1,17},{9,25},{17,1},{25,9},{2,18},{10... | collective-permute-start | bytes 1769480 | tf_op jit(solution)/shard_map/ppermute | solution.py:76
  638.1 23.8 %collective-permute-start.58 = (bf16[2,2,24,3072]{3,2,0,1:T(8,128)(2,1)S(1)}, bf16[2,2,24,3072]{3,2,0,1:T(8,128)(2,1)S(1)}, u32[]{:S(2)}, u32[]{:S(2)}) collective-permute-start(bf16[2,2,24,3072]{3,2,0,1:T(8,128)(2,1)S(1)} %bitcast.722), channel_id=1, source_target_pairs={{0,8},{8,0},{16,24},{24,16},{1,9},{9,1},{17,25},{25,17},{2,10},{10... | collective-permute-start | bytes 1769480 | tf_op jit(solution)/shard_map/ppermute | solution.py:76
  648.7 25.5 %collective-permute-start.73 = (bf16[2,96,768]{2,1,0:T(8,128)(2,1)S(1)}, bf16[2,96,768]{2,1,0:T(8,128)(2,1)S(1)}, u32[]{:S(2)}, u32[]{:S(2)}) collective-permute-start(bf16[2,96,768]{2,1,0:T(8,128)(2,1)S(1)} %dynamic-slice_bitcast_fusion.13), channel_id=1, source_target_pairs={{0,8},{8,0},{16,24},{24,16},{1,9},{9,1},{17,25},{25,17},{2,10},{10... | collective-permute-start | bytes 884744 | tf_op jit(solution)/shard_map/ppermute | solution.py:76
  650.8 26.3 %collective-permute-start.71 = (bf16[2,96,768]{2,1,0:T(8,128)(2,1)S(1)}, bf16[2,96,768]{2,1,0:T(8,128)(2,1)S(1)}, u32[]{:S(2)}, u32[]{:S(2)}) collective-permute-start(bf16[2,96,768]{2,1,0:T(8,128)(2,1)S(1)} %dynamic-slice_bitcast_fusion.14), channel_id=1, source_target_pairs={{0,16},{8,24},{16,0},{24,8},{1,17},{9,25},{17,1},{25,9},{2,18},{10... | collective-permute-start | bytes 884744 | tf_op jit(solution)/shard_map/ppermute | solution.py:76
  662.1 9.3 %collective-permute-start.59 = (bf16[2,24,3072]{2,1,0:T(8,128)(2,1)S(1)}, bf16[2,24,3072]{2,1,0:T(8,128)(2,1)S(1)}, u32[]{:S(2)}, u32[]{:S(2)}) collective-permute-start(bf16[2,24,3072]{2,1,0:T(8,128)(2,1)S(1)} %dynamic-slice_bitcast_fusion.16), channel_id=1, source_target_pairs={{0,16},{8,24},{16,0},{24,8},{1,17},{9,25},{17,1},{25,9},{2,18},{10... | collective-permute-start | bytes 884744 | tf_op jit(solution)/shard_map/ppermute | solution.py:76
  665.7 44.7 %collective-permute-start.48 = (bf16[2,2,32,3072]{3,2,1,0:T(8,128)(2,1)S(1)}, bf16[2,2,32,3072]{3,2,1,0:T(8,128)(2,1)S(1)}, u32[]{:S(2)}, u32[]{:S(2)}) collective-permute-start(bf16[2,2,32,3072]{3,2,1,0:T(8,128)(2,1)S(1)} %dynamic-slice_bitcast_fusion.4), channel_id=1, source_target_pairs={{0,16},{8,24},{16,0},{24,8},{1,17},{9,25},{17,1},{25,9},{2,18},{10... | collective-permute-start | bytes 2359304 | tf_op jit(solution)/shard_map/ppermute | solution.py:76
  674.2 10.8 %collective-permute-start.64 = (bf16[24,3072]{1,0:T(8,128)(2,1)S(1)}, bf16[24,3072]{1,0:T(8,128)(2,1)S(1)}, u32[]{:S(2)}, u32[]{:S(2)}) collective-permute-start(bf16[24,3072]{1,0:T(8,128)(2,1)S(1)} %get-tuple-element.339), channel_id=1, source_target_pairs={{0,6},{1,7},{2,0},{3,1},{4,2},{5,3},{6,4},{7,5},{8,14},{9,15},{10,... | collective-permute-start | bytes 442376 | tf_op jit(solution)/shard_map/ppermute | solution.py:126
  677.4 9.8 %collective-permute-start.74 = (bf16[96,768]{1,0:T(8,128)(2,1)S(1)}, bf16[96,768]{1,0:T(8,128)(2,1)S(1)}, u32[]{:S(2)}, u32[]{:S(2)}) collective-permute-start(bf16[96,768]{1,0:T(8,128)(2,1)S(1)} %get-tuple-element.330), channel_id=1, source_target_pairs={{0,2},{1,3},{2,4},{3,5},{4,6},{5,7},{6,0},{7,1},{8,10},{9,11},{10,... | collective-permute-start | bytes 442376 | tf_op jit(solution)/shard_map/ppermute | solution.py:126
  678.8 9.4 %collective-permute-start.75 = (bf16[96,768]{1,0:T(8,128)(2,1)S(1)}, bf16[96,768]{1,0:T(8,128)(2,1)S(1)}, u32[]{:S(2)}, u32[]{:S(2)}) collective-permute-start(bf16[96,768]{1,0:T(8,128)(2,1)S(1)} %get-tuple-element.331), channel_id=1, source_target_pairs={{0,4},{1,5},{2,6},{3,7},{4,0},{5,1},{6,2},{7,3},{8,12},{9,13},{10,... | collective-permute-start | bytes 442376 | tf_op jit(solution)/shard_map/ppermute | solution.py:126
  695.6 16.6 %collective-permute-start.46 = (bf16[2,2,32,3072]{3,2,0,1:T(8,128)(2,1)S(1)}, bf16[2,2,32,3072]{3,2,0,1:T(8,128)(2,1)S(1)}, u32[]{:S(2)}, u32[]{:S(2)}) collective-permute-start(bf16[2,2,32,3072]{3,2,0,1:T(8,128)(2,1)S(1)} %bitcast.719), channel_id=1, source_target_pairs={{0,8},{8,0},{16,24},{24,16},{1,9},{9,1},{17,25},{25,17},{2,10},{10... | collective-permute-start | bytes 2359304 | tf_op jit(solution)/shard_map/ppermute | solution.py:76
  697.0 28.9 %collective-permute-start.78 = (bf16[96,384]{1,0:T(8,128)(2,1)S(1)}, bf16[96,384]{1,0:T(8,128)(2,1)S(1)}, u32[]{:S(2)}, u32[]{:S(2)}) collective-permute-start(bf16[96,384]{1,0:T(8,128)(2,1)S(1)} %slice.331), channel_id=1, source_target_pairs={{0,16},{8,24},{16,0},{24,8},{1,17},{9,25},{17,1},{25,9},{2,18},{10... | collective-permute-start | bytes 221192 | tf_op jit(solution)/shard_map/ppermute | solution.py:76
  699.3 26.7 %collective-permute-start.80 = (bf16[96,384]{1,0:T(8,128)(2,1)S(1)}, bf16[96,384]{1,0:T(8,128)(2,1)S(1)}, u32[]{:S(2)}, u32[]{:S(2)}) collective-permute-start(bf16[96,384]{1,0:T(8,128)(2,1)S(1)} %slice.332), channel_id=1, source_target_pairs={{0,8},{8,0},{16,24},{24,16},{1,9},{9,1},{17,25},{25,17},{2,10},{10... | collective-permute-start | bytes 221192 | tf_op jit(solution)/shard_map/ppermute | solution.py:76
  700.0 9.1 %collective-permute-start.68 = (bf16[24,1536]{1,0:T(8,128)(2,1)S(1)}, bf16[24,1536]{1,0:T(8,128)(2,1)S(1)}, u32[]{:S(2)}, u32[]{:S(2)}) collective-permute-start(bf16[24,1536]{1,0:T(8,128)(2,1)S(1)} %slice.327), channel_id=1, source_target_pairs={{0,8},{8,0},{16,24},{24,16},{1,9},{9,1},{17,25},{25,17},{2,10},{10... | collective-permute-start | bytes 221192 | tf_op jit(solution)/shard_map/ppermute | solution.py:76
  710.7 8.4 %collective-permute-start.49 = (bf16[2,32,3072]{2,1,0:T(8,128)(2,1)S(1)}, bf16[2,32,3072]{2,1,0:T(8,128)(2,1)S(1)}, u32[]{:S(2)}, u32[]{:S(2)}) collective-permute-start(bf16[2,32,3072]{2,1,0:T(8,128)(2,1)S(1)} %dynamic-slice_bitcast_fusion.11), channel_id=1, source_target_pairs={{0,8},{8,0},{16,24},{24,16},{1,9},{9,1},{17,25},{25,17},{2,10},{10... | collective-permute-start | bytes 1179656 | tf_op jit(solution)/shard_map/ppermute | solution.py:76
  720.7 8.5 %collective-permute-start.50 = (bf16[32,3072]{1,0:T(8,128)(2,1)S(1)}, bf16[32,3072]{1,0:T(8,128)(2,1)S(1)}, u32[]{:S(2)}, u32[]{:S(2)}) collective-permute-start(bf16[32,3072]{1,0:T(8,128)(2,1)S(1)} %get-tuple-element.323), channel_id=1, source_target_pairs={{0,2},{1,3},{2,4},{3,5},{4,6},{5,7},{6,0},{7,1},{8,10},{9,11},{10,... | collective-permute-start | bytes 589832 | tf_op jit(solution)/shard_map/ppermute | solution.py:126
  723.2 10.1 %collective-permute-start.51 = (bf16[32,3072]{1,0:T(8,128)(2,1)S(1)}, bf16[32,3072]{1,0:T(8,128)(2,1)S(1)}, u32[]{:S(2)}, u32[]{:S(2)}) collective-permute-start(bf16[32,3072]{1,0:T(8,128)(2,1)S(1)} %get-tuple-element.324), channel_id=1, source_target_pairs={{0,4},{1,5},{2,6},{3,7},{4,0},{5,1},{6,2},{7,3},{8,12},{9,13},{10,... | collective-permute-start | bytes 589832 | tf_op jit(solution)/shard_map/ppermute | solution.py:126
  (122 other events, 866.6 us)
